TPU v7x, 32 devices: a whole 2x2x4 slice. The times are simulated.
32 devices in a mesh: seq: 8 (over z, x), dp: 4 (over y, core).
Axes of the slice: x: 2, y: 2, z: 4, core: 2. Of those that a mesh axis runs over, the one named last changes fastest.
Arguments:
- inputs: float32 [4, 2048, 768], P('dp', 'seq'), may hold values from -6 to 6
- doc_ids: int32 [4, 2048], P('dp'), may hold values from 0 to 1, as said below
- cotangent: float32 [4, 2048, 768], P('dp', 'seq'), may hold values from -6 to 6
- ln1_gain: bfloat16 [768], P(('seq', 'dp')), may hold values from 0.099609375 to 1.8984375
- ln1_shift: bfloat16 [768], P(('seq', 'dp')), may hold values from -3 to 3
- w_qkv: bfloat16 [768, 2304], P(('seq', 'dp')), may hold values from -0.21875 to 0.21875
- b_query: bfloat16 [768], P(('seq', 'dp')), may hold values from -3 to 3
- b_value: bfloat16 [768], P(('seq', 'dp')), may hold values from -3 to 3
- w_attn_out: bfloat16 [768, 768], P(('seq', 'dp')), may hold values from -1.75 to 1.75
- b_attn_out: bfloat16 [768], P(('seq', 'dp')), may hold values from -3 to 3
- ln2_gain: bfloat16 [768], P(('seq', 'dp')), may hold values from 0.099609375 to 1.8984375
- ln2_shift: bfloat16 [768], P(('seq', 'dp')), may hold values from -3 to 3
- w_fc: bfloat16 [768, 3072], P(('seq', 'dp')), may hold values from -0.21875 to 0.21875
- b_fc: bfloat16 [3072], P(('seq', 'dp')), may hold values from -3 to 3
- w_mlp_out: bfloat16 [3072, 768], P(('seq', 'dp')), may hold values from -0.109375 to 0.109375
- b_mlp_out: bfloat16 [768], P(('seq', 'dp')), may hold values from -3 to 3
Outputs:
- result: float32 [4, 2048, 768], P('dp', 'seq')
- grad_inputs: float32 [4, 2048, 768], P('dp', 'seq')
- grad_ln1_gain: float32 [768], P(('seq', 'dp'))
- grad_ln1_shift: float32 [768], P(('seq', 'dp'))
- grad_w_qkv: float32 [768, 2304], P(('seq', 'dp'))
- grad_b_query: float32 [768], P(('seq', 'dp'))
- grad_b_value: float32 [768], P(('seq', 'dp'))
- grad_w_attn_out: float32 [768, 768], P(('seq', 'dp'))
- grad_b_attn_out: float32 [768], P(('seq', 'dp'))
- grad_ln2_gain: float32 [768], P(('seq', 'dp'))
- grad_ln2_shift: float32 [768], P(('seq', 'dp'))
- grad_w_fc: float32 [768, 3072], P(('seq', 'dp'))
- grad_b_fc: float32 [3072], P(('seq', 'dp'))
- grad_w_mlp_out: float32 [3072, 768], P(('seq', 'dp'))
- grad_b_mlp_out: float32 [768], P(('seq', 'dp'))
Inputs may be any that keep to these rules, and one draw needn't show every extreme that they name: `doc_ids`: within each group, document numbers never fall and start at 0. Every group holds two documents: one of exactly 1792 tokens and one of 256 tokens, in either order, so the boundary falls at 256 or at 1792.
All inputs are finite; a program needn't handle non-finite values.
Results may differ from a plain program's by a relative error of at most 0.019.
Values may be sent and summed in bfloat16 or wider, within the bound.
No kernel may reach another device: no remote copies, remote signals or barrier semaphores. Data moves between devices by JAX's collectives and lax.ppermute only.
A program may use at most 192 MiB of HBM per device.

v0:
```python
import functools

import jax
import jax.numpy as jnp
from jax import lax
from jax.experimental import pallas as pl
from jax.experimental.pallas import tpu as pltpu
from jax.sharding import PartitionSpec as P


HEADS = 12
LANES = 128

norm_eps = 1e-05
gelu_root = 0.7978845608028654
gelu_cube = 0.044715
score_scale = 0.125
hidden_score = -1e30


bf16 = jnp.bfloat16
f32 = jnp.float32


def layer_norm(values, gain, shift):
    average = jnp.mean(values, axis=-1, keepdims=True)
    centred = values - average
    variance = jnp.mean(centred * centred, axis=-1, keepdims=True)
    inverse = lax.rsqrt(variance + norm_eps)
    normed = centred * inverse
    return (normed * gain + shift, normed, inverse)


def norm_back(grad_out, normed, inverse, gain):
    scaled = grad_out * gain
    first = jnp.mean(scaled, axis=-1, keepdims=True)
    second = jnp.mean(scaled * normed, axis=-1, keepdims=True)
    return inverse * (scaled - first - normed * second)


def gelu_pair(values):
    inner = gelu_root * (values + gelu_cube * values * values * values)
    tangent = jnp.tanh(inner)
    output = 0.5 * values * (1.0 + tangent)
    slope = 0.5 * (1.0 + tangent) + 0.5 * values * (1.0 - tangent * tangent) * gelu_root * (
        1.0 + 3.0 * gelu_cube * values * values
    )
    return (output, slope)


def dot(left, right, left_dim, right_dim):
    return lax.dot_general(
        left, right, (((left_dim,), (right_dim,)), ((), ())), preferred_element_type=f32
    )


def bits_of(sizes):
    out = []
    for axis in ("seq", "dp"):
        bit = sizes[axis] // 2
        while bit >= 1:
            out.append((axis, bit))
            bit //= 2
    return out


def step_orders(sizes):
    order = bits_of(sizes)
    seq_bits = [s for s in order if s[0] == "seq"]
    dp_bits = [s for s in order if s[0] == "dp"]
    far, near = seq_bits[:-1], seq_bits[-1:]
    side, core = dp_bits[:-1], dp_bits[-1:]
    return (far + near + side + core, far + side + near + core)


def own_bit(step):
    axis, bit = step
    return (lax.axis_index(axis) // bit) % 2


def exchange(value, step, sizes):
    axis, bit = step
    return lax.ppermute(value, axis, [(i, i ^ bit) for i in range(sizes[axis])])


def gather(shard, steps, sizes, join=True):
    place = {step: n for n, step in enumerate(bits_of(sizes))}
    have, value = [], shard
    for n, step in enumerate(steps):
        other = exchange(value, step, sizes)
        if n == len(steps) - 1 and not join:
            return (value.reshape((-1,) + shard.shape), other.reshape((-1,) + shard.shape))
        at = sum(1 for m in have if m < place[step])
        have.append(place[step])
        mine, other = jnp.expand_dims(value, at), jnp.expand_dims(other, at)
        shape = mine.shape[:at] + (2,) + mine.shape[at + 1 :]
        side = lax.broadcasted_iota(jnp.int32, shape, at)
        value = jnp.where(side == own_bit(step), mine, other)
    return value.reshape(-1, shard.shape[1])


def scatter_sum(full, steps, sizes):
    order = bits_of(sizes)
    count = 2 ** len(order)
    value = full.reshape((2,) * len(order) + (full.shape[0] // count,) + full.shape[1:])
    left = list(order)
    for step in reversed(steps):
        at = left.index(step)
        left.remove(step)
        low = lax.index_in_dim(value, 0, at, keepdims=False)
        high = lax.index_in_dim(value, 1, at, keepdims=False)
        upper = own_bit(step) == 1
        got = exchange(jnp.where(upper, low, high), step, sizes)
        value = jnp.where(upper, high, low).astype(f32) + got.astype(f32)
        if left:
            value = value.astype(bf16)
    return value


def scatter_sorted(send, keep, steps, sizes):
    for n, step in enumerate(reversed(steps)):
        got = exchange(send, step, sizes)
        total = keep.astype(f32) + got.astype(f32)
        if n < len(steps) - 1:
            rows = total.shape[0] // 2
            send, keep = total[:rows].astype(bf16), total[rows:].astype(bf16)
    return total


def send_order(steps, sizes, width):
    order = bits_of(sizes)
    count = len(order)
    rows = width // 2**count
    column = lax.broadcasted_iota(jnp.int32, (1, width), 1)
    at, inside = column // rows, column % rows
    owner = lax.axis_index("seq") * sizes["dp"] + lax.axis_index("dp")
    for n, step in enumerate(reversed(steps)):
        other = 1 - (at >> (count - 1 - n)) % 2
        owner = owner ^ (other << (count - 1 - order.index(step)))
    row = lax.broadcasted_iota(jnp.int32, (width, width), 0)
    return (row == owner * rows + inside).astype(bf16)


def block_slot(far_pos, index, far):
    return lax.rem(far_pos - index + far, far)


def triangle(size):
    key_pos = lax.broadcasted_iota(jnp.int32, (size, size), 0)
    query_pos = lax.broadcasted_iota(jnp.int32, (size, size), 1)
    return jnp.where(key_pos <= query_pos, 0.0, hidden_score)


def forward_kernel(heads, dim, far, where_ref, *refs):
    query_refs, key_refs, pair_refs = refs[:far], refs[far : 2 * far], refs[2 * far : 3 * far]
    own_ref, pair_ref, out_ref, lse_ref = refs[3 * far : 3 * far + 4]
    slot_refs, tri_ref = refs[3 * far + 4 : 4 * far + 4], refs[4 * far + 4]
    far_pos, near_pos = where_ref[0], where_ref[1]
    rows = heads * dim
    for s in range(far):
        own_ref[s, :rows, :] = query_refs[s][...]
        own_ref[s, rows:, :] = key_refs[s][...]
        pair_ref[s] = pair_refs[s][...]
    tri_ref[0] = jnp.zeros(tri_ref.shape[1:], f32)
    tri_ref[1] = triangle(tri_ref.shape[1])

    def head_rows(part, head):
        return pl.ds(part * rows + head * dim, dim)

    def query_block(j, _):
        first = where_ref[2 + j]
        slot_j = block_slot(far_pos, j, far)
        queries = [
            own_ref[slot_j, head_rows(0, h), :] * jnp.asarray(score_scale, bf16)
            for h in range(heads)
        ]

        def tiles(i, state):
            slot_i = block_slot(far_pos, i, far)
            own_at, pair_at = 2 * i + near_pos, 2 * i + 1 - near_pos
            own_bias = jnp.where(own_at >= first, 0.0, hidden_score)
            diagonal = (i == j).astype(jnp.int32)
            pair_seen = (pair_at >= first) & (pair_at < 2 * j + near_pos)
            pair_bias = jnp.where(pair_seen, 0.0, hidden_score)
            out = []
            for h in range(heads):
                top, total, acc = state[h]
                own = dot(own_ref[slot_i, head_rows(1, h), :], queries[h], 0, 0)
                own = own + tri_ref[diagonal] + own_bias
                pair = dot(pair_ref[slot_i, head_rows(0, h), :], queries[h], 0, 0) + pair_bias
                new_top = jnp.maximum(top, jnp.max(jnp.maximum(own, pair), axis=0, keepdims=True))
                own = jnp.exp(own - new_top)
                pair = jnp.exp(pair - new_top)
                shrink = jnp.exp(top - new_top)
                total = total * shrink + jnp.sum(own + pair, axis=0, keepdims=True)
                acc = (
                    acc * shrink
                    + dot(own_ref[slot_i, head_rows(2, h), :], own.astype(bf16), 1, 0)
                    + dot(pair_ref[slot_i, head_rows(1, h), :], pair.astype(bf16), 1, 0)
                )
                out.append((new_top, total, acc))
            return tuple(out)

        size = own_ref.shape[2]
        state = tuple(
            (
                jnp.full((1, size), hidden_score, f32),
                jnp.zeros((1, size), f32),
                jnp.zeros((dim, size), f32),
            )
            for _ in range(heads)
        )
        state = lax.fori_loop(first // 2, j + 1, tiles, state)
        for h in range(heads):
            top, total, acc = state[h]
            done = acc / total
            out_ref[slot_j, pl.ds(h * dim, dim), :] = done
            lse_ref[slot_j, pl.ds(h, 1), :] = top + jnp.log(total)
        return 0

    lax.fori_loop(0, far, query_block, 0)
    for s in range(far):
        slot_refs[s][...] = out_ref[s].astype(bf16)


def backward_kernel(heads, dim, far, where_ref, own_ref, pair_ref, out_ref, lse_ref, *refs):
    grad_refs, query_refs, pair_grad_refs = refs[:far], refs[far : 2 * far], refs[2 * far : 3 * far]
    own_grad_ref, grad_ref, query_ref, tri_ref, acc_ref = refs[3 * far :]
    far_pos, near_pos = where_ref[0], where_ref[1]
    rows = heads * dim
    for s in range(far):
        grad_ref[s] = grad_refs[s][...]
    tri_ref[0] = jnp.zeros(tri_ref.shape[1:], f32)
    tri_ref[1] = triangle(tri_ref.shape[1])
    own_grad_ref[...] = jnp.zeros(own_grad_ref.shape, f32)
    acc_ref[...] = jnp.zeros(acc_ref.shape, f32)

    def head_rows(part, head):
        return pl.ds(part * rows + head * dim, dim)

    def query_block(j, _):
        first = where_ref[2 + j]
        slot_j = block_slot(far_pos, j, far)
        queries = [
            own_ref[slot_j, head_rows(0, h), :] * jnp.asarray(score_scale, bf16)
            for h in range(heads)
        ]
        grads = [grad_ref[slot_j, head_rows(0, h), :] for h in range(heads)]
        deltas = [
            jnp.sum(grads[h].astype(f32) * out_ref[slot_j, head_rows(0, h), :], axis=0, keepdims=True)
            for h in range(heads)
        ]
        lses = [lse_ref[slot_j, pl.ds(h, 1), :] for h in range(heads)]

        def tile(h, keys, vals, bias, mask, into, slot_i):
            scores = dot(keys, queries[h], 0, 0)
            if mask is not None:
                scores = scores + tri_ref[mask]
            prob = jnp.exp(scores - (lses[h] - bias))
            grad_prob = dot(vals, grads[h], 0, 0)
            grad_score = (prob * (grad_prob - deltas[h])).astype(bf16)
            into[slot_i, head_rows(0, h), :] += dot(queries[h], grad_score, 1, 1)
            into[slot_i, head_rows(1, h), :] += dot(grads[h], prob.astype(bf16), 1, 1)
            return dot(keys, grad_score, 1, 0)

        def tiles(i, state):
            slot_i = block_slot(far_pos, i, far)
            own_at, pair_at = 2 * i + near_pos, 2 * i + 1 - near_pos
            own_bias = jnp.where(own_at >= first, 0.0, hidden_score)
            diagonal = (i == j).astype(jnp.int32)
            pair_seen = (pair_at >= first) & (pair_at < 2 * j + near_pos)
            pair_bias = jnp.where(pair_seen, 0.0, hidden_score)
            out = []
            for h in range(heads):
                own = tile(
                    h,
                    own_ref[slot_i, head_rows(1, h), :],
                    own_ref[slot_i, head_rows(2, h), :],
                    own_bias,
                    diagonal,
                    own_grad_ref,
                    slot_i,
                )
                pair = tile(
                    h,
                    pair_ref[slot_i, head_rows(0, h), :],
                    pair_ref[slot_i, head_rows(1, h), :],
                    pair_bias,
                    None,
                    acc_ref,
                    slot_i,
                )
                out.append(state[h] + own + pair)
            return tuple(out)

        size = own_ref.shape[2]
        state = tuple(jnp.zeros((dim, size), f32) for _ in range(heads))
        state = lax.fori_loop(first // 2, j + 1, tiles, state)
        for h in range(heads):
            query_ref[slot_j, head_rows(0, h), :] = (state[h] * score_scale).astype(bf16)
        return 0

    lax.fori_loop(0, far, query_block, 0)
    for s in range(far):
        query_refs[s][...] = query_ref[s]
        pair_grad_refs[s][...] = acc_ref[s].astype(bf16)


def vmem():
    return pl.BlockSpec(memory_space=pltpu.VMEM)


def attend(where, queries, keys, pairs, heads, dim):
    far, size, rows = len(queries), queries[0].shape[1], heads * dim
    return pl.pallas_call(
        functools.partial(forward_kernel, heads, dim, far),
        name="attend",
        out_shape=(
            jax.ShapeDtypeStruct((far, 3 * rows, size), bf16),
            jax.ShapeDtypeStruct((far, 2 * rows, size), bf16),
            jax.ShapeDtypeStruct((far, rows, size), f32),
            jax.ShapeDtypeStruct((far, 8, size), f32),
        )
        + (jax.ShapeDtypeStruct((rows, size), bf16),) * far,
        in_specs=[pl.BlockSpec(memory_space=pltpu.SMEM)] + [vmem()] * (3 * far),
        out_specs=(vmem(),) * (4 + far),
        scratch_shapes=[pltpu.VMEM((2, size, size), f32)],
        cost_estimate=pl.CostEstimate(
            flops=16 * heads * 4 * dim * size * size,
            bytes_accessed=24 * far * rows * size,
            transcendentals=16 * heads * size * size,
        ),
    )(where, *queries, *keys, *pairs)


def attend_back(where, own, pair, out, lse, grads, heads, dim):
    far, size, rows = len(grads), own.shape[2], heads * dim
    return pl.pallas_call(
        functools.partial(backward_kernel, heads, dim, far),
        name="attend_back",
        out_shape=(jax.ShapeDtypeStruct((rows, size), bf16),) * far
        + (jax.ShapeDtypeStruct((2 * rows, size), bf16),) * far
        + (jax.ShapeDtypeStruct((far, 2 * rows, size), f32),),
        in_specs=[pl.BlockSpec(memory_space=pltpu.SMEM)] + [vmem()] * (4 + far),
        out_specs=(vmem(),) * (2 * far + 1),
        scratch_shapes=[
            pltpu.VMEM((far, rows, size), bf16),
            pltpu.VMEM((far, rows, size), bf16),
            pltpu.VMEM((2, size, size), f32),
            pltpu.VMEM((far, 2 * rows, size), f32),
        ],
        cost_estimate=pl.CostEstimate(
            flops=16 * heads * 10 * dim * size * size,
            bytes_accessed=32 * far * rows * size,
            transcendentals=16 * heads * size * size,
        ),
    )(where, own, pair, out, lse, *grads)


def project_kernel(rows, far, where_ref, tokens_ref, one_ref, two_ref, normed_ref, small_ref, *refs):
    query_refs, key_refs, all_ref = refs[:far], refs[far : 2 * far], refs[2 * far]
    width, half = tokens_ref.shape[1], one_ref.shape[1]
    columns = two_ref[:, half:].astype(f32)
    small = columns.T[: small_ref.shape[0]]
    small_ref[...] = small
    normed = layer_norm(tokens_ref[...], small[0:1], small[1:2])[0].astype(bf16)
    normed_ref[...] = normed
    one = dot(one_ref[...], normed, 0, 1)
    all_ref[:width, :] = (one[:width] + columns[:, 2:3]).astype(bf16)
    all_ref[width:half, :] = one[width:].astype(bf16)
    two = dot(two_ref[:, :half], normed, 0, 1)
    cut = 2 * width - half
    all_ref[half : 2 * width, :] = two[:cut].astype(bf16)
    all_ref[2 * width :, :] = (two[cut:] + columns[:, 3:4]).astype(bf16)
    for s in range(far):
        first = lax.rem(where_ref[0] + s, far) * rows
        for part, ref, at in ((0, query_refs[s], 0), (1, key_refs[s], 0), (2, key_refs[s], rows)):
            start = pl.multiple_of(part * width + first, rows)
            ref[pl.ds(at, rows), :] = all_ref[pl.ds(start, rows), :]


def project(where, tokens, one, two, rows, far):
    size, width = tokens.shape
    return pl.pallas_call(
        functools.partial(project_kernel, rows, far),
        name="project",
        out_shape=(
            jax.ShapeDtypeStruct((size, width), bf16),
            jax.ShapeDtypeStruct((8, width), f32),
        )
        + (jax.ShapeDtypeStruct((rows, size), bf16),) * far
        + (jax.ShapeDtypeStruct((2 * rows, size), bf16),) * far,
        in_specs=[pl.BlockSpec(memory_space=pltpu.SMEM)] + [vmem()] * 3,
        out_specs=(vmem(),) * (2 + 2 * far),
        scratch_shapes=[pltpu.VMEM((3 * width, size), bf16)],
        cost_estimate=pl.CostEstimate(
            flops=6 * size * width * width, bytes_accessed=12 * width * width, transcendentals=0
        ),
    )(where, tokens, one, two)


def middle_kernel(rows, far, pieces, where_ref, tokens_ref, cot_ref, *refs):
    slot_refs = refs[:far]
    proj_ref, small_ref, fc_ref, fc_bias_ref = refs[far : far + 4]
    out_refs = refs[far + 4 : far + 4 + pieces]
    refs = refs[far + 4 + pieces :]
    (result_ref, att_ref, mlp_ref, resid_ref, grad_resid_ref, sums_ref) = refs[:6]
    hidden_ref, hidden_grad_ref, fc_sum_ref = refs[6:9]
    grad_refs = refs[9 : 9 + far]
    normal_ref, inverse_ref, acc_ref, cot_bf_ref, back_ref, out_ref = refs[9 + far :]
    step = pl.program_id(0)

    @pl.when(step == 0)
    def _():
        for s in range(far):
            first = pl.multiple_of(lax.rem(where_ref[0] + s, far) * rows, rows)
            att_ref[pl.ds(first, rows), :] = slot_refs[s][...]
        resid = tokens_ref[...] + dot(att_ref[...], proj_ref[...], 0, 0) + small_ref[4:5]
        normed, normal, inverse = layer_norm(resid, small_ref[5:6], small_ref[6:7])
        mlp_ref[...] = normed.astype(bf16)
        normal_ref[...] = normal
        inverse_ref[...] = jnp.broadcast_to(inverse, inverse_ref.shape)
        result_ref[...] = resid + small_ref[7:8]
        cot_bf_ref[...] = cot_ref[...].astype(bf16)
        acc_ref[...] = jnp.zeros(acc_ref.shape, f32)

    weight_in = fc_ref[...]
    if pieces == 1:
        weight_out = out_refs[0][...]
    else:
        count, piece = out_refs[0].shape[:2]
        for side, ref in enumerate(out_refs):
            core = (where_ref[2 + far] + side) % 2
            for n in range(count):
                start = pl.multiple_of((2 * n + core) * piece, 32)
                out_ref[pl.ds(start, piece), :] = ref[n]
        weight_out = out_ref[...]
    pre = dot(mlp_ref[...], weight_in, 1, 0) + fc_bias_ref[...]
    act, slope = gelu_pair(pre)
    hidden = act.astype(bf16)
    hidden_ref[...] = hidden
    result_ref[...] += dot(hidden, weight_out, 1, 0)
    grad = dot(cot_bf_ref[...], weight_out, 1, 1) * slope
    fc_sum_ref[...] = jnp.sum(grad, axis=0, keepdims=True)
    grad = grad.astype(bf16)
    hidden_grad_ref[...] = grad
    acc_ref[...] += dot(grad, weight_in, 1, 1)

    @pl.when(step == pl.num_programs(0) - 1)
    def _():
        normal, grad_mid, cot = normal_ref[...], acc_ref[...], cot_ref[...]
        back = norm_back(grad_mid, normal, inverse_ref[:, 0:1], small_ref[5:6])
        grad_resid = cot + back
        grad_resid_ref[...] = grad_resid
        resid_bf = grad_resid.astype(bf16)
        resid_ref[...] = resid_bf
        back_ref[...] = dot(proj_ref[...], resid_bf, 1, 1).astype(bf16)
        for s in range(far):
            first = pl.multiple_of(lax.rem(where_ref[0] + s, far) * rows, rows)
            grad_refs[s][...] = back_ref[pl.ds(first, rows), :]
        totals = (grad_resid, grad_mid * normal, grad_mid, cot)
        sums_ref[0:4, :] = jnp.concatenate(
            [jnp.sum(value, axis=0, keepdims=True) for value in totals], axis=0
        )
        sums_ref[4:8, :] = jnp.zeros((4, sums_ref.shape[1]), f32)


def middle(where, tokens, cot, slots, fc_proj, small, out, fc_bias, rows):
    far, (size, width), hidden = len(slots), tokens.shape, fc_bias.shape[1]
    cut = width
    steps = hidden // cut

    def whole(shape):
        return pl.BlockSpec(shape, lambda f: (0,) * len(shape))

    token_spec, rows_spec = whole((size, width)), whole((rows, size))
    hidden_spec = pl.BlockSpec((size, cut), lambda f: (0, f))
    bias_spec = pl.BlockSpec((1, cut), lambda f: (0, f))
    if len(out) == 1:
        out_specs = [pl.BlockSpec((cut, width), lambda f: (f, 0))]
    else:
        piece = out[0].shape[1]
        out_specs = [pl.BlockSpec((cut // piece // 2, piece, width), lambda f: (f, 0, 0))] * 2
    return pl.pallas_call(
        functools.partial(middle_kernel, rows, far, len(out)),
        name="middle",
        grid=(steps,),
        out_shape=(
            jax.ShapeDtypeStruct((size, width), f32),
            jax.ShapeDtypeStruct((width, size), bf16),
            jax.ShapeDtypeStruct((size, width), bf16),
            jax.ShapeDtypeStruct((size, width), bf16),
            jax.ShapeDtypeStruct((size, width), f32),
            jax.ShapeDtypeStruct((8, width), f32),
            jax.ShapeDtypeStruct((size, hidden), bf16),
            jax.ShapeDtypeStruct((size, hidden), bf16),
            jax.ShapeDtypeStruct((1, hidden), f32),
        )
        + (jax.ShapeDtypeStruct((rows, size), bf16),) * far,
        in_specs=[pl.BlockSpec(memory_space=pltpu.SMEM), token_spec, token_spec]
        + [rows_spec] * far
        + [
            pl.BlockSpec((width, width), lambda f: (0, hidden // width)),
            whole((8, width)),
            pl.BlockSpec((width, cut), lambda f: (0, f)),
            bias_spec,
        ]
        + out_specs,
        out_specs=(
            token_spec,
            whole((width, size)),
            token_spec,
            token_spec,
            token_spec,
            whole((8, width)),
            hidden_spec,
            hidden_spec,
            bias_spec,
        )
        + (rows_spec,) * far,
        scratch_shapes=[
            pltpu.VMEM((size, width), f32),
            pltpu.VMEM((size, LANES), f32),
            pltpu.VMEM((size, width), f32),
            pltpu.VMEM((size, width), bf16),
            pltpu.VMEM((width, size), bf16),
            pltpu.VMEM((cut, width), bf16),
        ],
        cost_estimate=pl.CostEstimate(
            flops=8 * size * width * hidden + 4 * size * width * width,
            bytes_accessed=4 * width * hidden + 4 * size * hidden + 24 * size * width,
            transcendentals=size * hidden,
        ),
    )(where, tokens, cot, *slots, fc_proj, small, fc_proj, fc_bias, *out)


def per_device(
    sizes,
    inputs,
    doc_ids,
    cotangent,
    ln1_gain,
    ln1_shift,
    w_qkv,
    b_query,
    b_value,
    w_attn_out,
    b_attn_out,
    ln2_gain,
    ln2_shift,
    w_fc,
    b_fc,
    w_mlp_out,
    b_mlp_out,
):
    order_one, order_two = step_orders(sizes)
    tokens = inputs[0]
    grad_out = cotangent[0]
    group_docs = doc_ids[0]
    tok_count, width = tokens.shape
    dim = width // HEADS
    seq = sizes["seq"]
    far = seq // 2
    heads = HEADS // far
    rows = heads * dim
    position = lax.axis_index("seq")
    far_pos, near_pos = position // 2, position % 2

    shard_rows = w_qkv.shape[0]
    vectors = [ln1_gain, ln1_shift, b_query, b_value, b_attn_out, ln2_gain, ln2_shift, b_mlp_out]
    fc_rows = b_fc.shape[0] // shard_rows
    vectors += [b_fc[n * shard_rows : (n + 1) * shard_rows] for n in range(fc_rows)]
    zero = jnp.zeros((), bf16)
    small = sum(
        lax.pad(v[None], zero, ((n, len(vectors) - 1 - n, 0), (0, 0, 0)))
        for n, v in enumerate(vectors)
    ).T
    small_count = small.shape[1]
    small = jnp.pad(small, ((0, 0), (0, LANES - small_count)))
    half = w_qkv.shape[1] // 2

    qkv_one = gather(w_qkv[:, :half], order_one, sizes)
    qkv_two = gather(jnp.concatenate([w_qkv[:, half:], small], axis=1), order_two, sizes)
    fc_proj_full = gather(jnp.concatenate([w_fc, w_attn_out], axis=1), order_one, sizes)
    out_aligned = w_mlp_out.shape[0] % 32 == 0
    out_full = gather(w_mlp_out, order_two, sizes, join=not out_aligned)
    if not out_aligned:
        out_full = (out_full,)

    fc_bias = qkv_two[:, half + 8 : half + small_count].astype(f32)
    fc_bias = fc_bias.reshape(-1, shard_rows, fc_rows).swapaxes(1, 2).reshape(1, -1)

    block_docs = group_docs[::tok_count]
    own_blocks = 2 * jnp.arange(far, dtype=jnp.int32) + near_pos
    own_docs = jnp.take(block_docs, own_blocks)
    first_blocks = jnp.sum(
        (block_docs[None, :] < own_docs[:, None]).astype(jnp.int32), axis=1, dtype=jnp.int32
    )
    core_bit = own_bit(bits_of(sizes)[-1])
    where = jnp.concatenate(
        [jnp.stack([far_pos, near_pos]), first_blocks, jnp.stack([core_bit])]
    ).astype(jnp.int32)

    def shift_far(value, shift):
        return lax.ppermute(
            value, "seq", [(i, (i + 2 * shift) % seq) for i in range(seq)]
        )

    def spread(slots):
        out = [slots[0]]
        for s in range(1, far):
            out.append(shift_far(slots[s], s))
        return out

    def collect(slots):
        out = [slots[0]]
        for s in range(1, far):
            out.append(shift_far(slots[s], far - s))
        return out

    def in_order(slots):
        stacked = jnp.stack(slots)
        return jnp.concatenate(
            [
                lax.dynamic_index_in_dim(stacked, lax.rem(g - far_pos + far, far), 0, keepdims=False)
                for g in range(far)
            ]
        )

    def to_pair(value):
        return lax.ppermute(value, "seq", [(i, i ^ 1) for i in range(seq)])

    attn_in, small, *slots = project(where, tokens, qkv_one, qkv_two, rows, far)
    key_slots = spread(slots[far:])
    query_slots = spread(slots[:far])
    pair_slots = []
    for value in key_slots:
        pair_slots.append(to_pair(value))
    own, pair, head_out, lse, *out_slots = attend(
        where, query_slots, key_slots, pair_slots, heads, dim
    )
    out_slots = collect(out_slots)
    (
        result,
        attended_t,
        mlp_in,
        resid_bf,
        grad_resid,
        middle_sums,
        hidden_bf,
        hidden_grad_bf,
        g_fc_b,
        *grad_slots,
    ) = middle(
        where, tokens, grad_out, out_slots, fc_proj_full, small, out_full, fc_bias, rows
    )
    grad_slots = spread(grad_slots)
    grad_bf = grad_out.astype(bf16)
    sort_one, sort_two = (send_order(o, sizes, width) for o in (order_one, order_two))
    part = width // 2

    g_out_w = dot(hidden_bf, grad_bf, 0, 0).astype(bf16)
    g_out_w = scatter_sum(g_out_w, order_two, sizes)
    both_sorted = dot(jnp.concatenate([mlp_in, attn_in]), sort_one, 1, 0).astype(bf16)
    mlp_sorted, sorted_one = both_sorted[:tok_count], both_sorted[tok_count:]
    att_sorted = dot(sort_one, attended_t, 0, 0).astype(bf16)
    fc_cols = hidden_grad_bf.shape[1]

    def fc_proj(low, high):
        g_fc = dot(mlp_sorted[:, low:high], hidden_grad_bf, 0, 0).astype(bf16)
        g_proj = dot(att_sorted[low:high], resid_bf, 1, 0).astype(bf16)
        return jnp.concatenate([g_fc, g_proj], axis=1)

    g_fc_proj = scatter_sorted(fc_proj(0, part), fc_proj(part, width), order_one, sizes)

    *back_slots, own_back = attend_back(
        where, own, pair, head_out, lse, grad_slots, heads, dim
    )
    from_pair = []
    for n in range(far):
        from_pair.append(to_pair(back_slots[far + n]))
    query_grad = in_order(collect(back_slots[:far]))
    key_slots = [(own_back[s] + from_pair[s].astype(f32)).astype(bf16) for s in range(far)]
    key_slots = collect(key_slots)
    qkv_grad_t = jnp.concatenate(
        [
            query_grad,
            in_order([v[:rows] for v in key_slots]),
            in_order([v[rows:] for v in key_slots]),
        ],
        axis=0,
    )
    sorted_two = dot(attn_in, sort_two, 1, 0).astype(bf16)
    g_qkv_one = [
        dot(sorted_one[:, low : low + part], qkv_grad_t[:half], 0, 1).astype(bf16)
        for low in (0, part)
    ]
    g_qkv_one = scatter_sorted(*g_qkv_one, order_one, sizes)
    grad_first = dot(qkv_grad_t[:half], qkv_one, 0, 1) + dot(
        qkv_grad_t[half:], qkv_two[:, :half], 0, 1
    )
    g_query_b = jnp.sum(qkv_grad_t[:width].astype(f32), axis=1, keepdims=True)
    g_value_b = jnp.sum(qkv_grad_t[2 * width :].astype(f32), axis=1, keepdims=True)
    gain_one = small[0:1]
    late_tokens, grad_first = lax.optimization_barrier((tokens, grad_first))
    _, normal_one, inverse_one = layer_norm(late_tokens, gain_one, gain_one)
    g_gain_one = jnp.sum(grad_first * normal_one, axis=0)
    g_shift_one = jnp.sum(grad_first, axis=0)
    grad_input = grad_resid + norm_back(grad_first, normal_one, inverse_one, gain_one)

    row_sums = jnp.concatenate([g_gain_one[None], g_shift_one[None], middle_sums[:4]]).T
    sums = jnp.concatenate([row_sums, g_query_b, g_value_b, g_fc_b.reshape(width, -1)], axis=1)
    sums = jnp.pad(sums, ((0, 0), (0, LANES - sums.shape[1]))).astype(bf16)
    sums = dot(sort_two, sums, 0, 0).astype(bf16)

    def qkv_sums(low, high):
        g_two = dot(sorted_two[:, low:high], qkv_grad_t[half:], 0, 1).astype(bf16)
        return jnp.concatenate([g_two, sums[low:high]], axis=1)

    g_qkv_two = scatter_sorted(qkv_sums(0, part), qkv_sums(part, width), order_two, sizes)
    g_qkv_two, sums = g_qkv_two[:, :half], g_qkv_two[:, half:]
    return (
        result[None],
        grad_input[None],
        sums[:, 0],
        sums[:, 1],
        jnp.concatenate([g_qkv_one, g_qkv_two], axis=1),
        sums[:, 6],
        sums[:, 7],
        g_fc_proj[:, fc_cols:],
        sums[:, 2],
        sums[:, 3],
        sums[:, 4],
        g_fc_proj[:, :fc_cols],
        sums[:, 8:small_count].reshape(-1),
        g_out_w,
        sums[:, 5],
    )


def solution(mesh):
    vector, matrix = P(("seq", "dp")), P(("seq", "dp"), None)
    block = P("dp", "seq", None)
    in_specs = (
        block,
        P("dp", None),
        block,
        vector,
        vector,
        matrix,
        vector,
        vector,
        matrix,
        vector,
        vector,
        vector,
        matrix,
        vector,
        matrix,
        vector,
    )
    out_specs = (
        block,
        block,
        vector,
        vector,
        matrix,
        vector,
        vector,
        matrix,
        vector,
        vector,
        vector,
        matrix,
        vector,
        matrix,
        vector,
    )

    def body(*args):
        return per_device(dict(mesh.shape), *args)

    return jax.shard_map(body, mesh=mesh, in_specs=in_specs, out_specs=out_specs, check_vma=False)
```

profile of v0, /device:TPU:0, one launch (start us, length us, event | category | flops | bytes accessed | tf_op | source)
XLA Modules:
  0.0 431.1 jit_solution(6912101589011183290)
XLA Ops:
  2.4 4.1 collective-permute-start.23
  12.2 11.8 %collective-permute-done = bf16[24,1152]{1,0:T(8,128)(2,1)S(1)} collective-permute-done((bf16[24,1152]{1,0:T(8,128)(2,1)S(1)}, bf16[24,1152]{1,0:T(8,128)(2,1)S(1)}, u32[]{:S(2)}, u32[]{:S(2)}) %collective-permute-start) | collective-permute-done | bytes 55328 | tf_op jit(solution)/shard_map/ppermute | solution.py:83
  26.6 11.4 %collective-permute-done.24 = bf16[2,24,3840]{2,1,0:T(8,128)(2,1)S(1)} collective-permute-done((bf16[2,24,3840]{2,1,0:T(8,128)(2,1)S(1)}, bf16[2,24,3840]{2,1,0:T(8,128)(2,1)S(1)}, u32[]{:S(2)}, u32[]{:S(2)}) %collective-permute-start.24) | collective-permute-done | bytes 368672 | tf_op jit(solution)/shard_map/ppermute | solution.py:83
  40.6 5.9 %collective-permute-done.29 = bf16[2,96,768]{2,1,0:T(8,128)(2,1)S(1)} collective-permute-done((bf16[2,96,768]{2,1,0:T(8,128)(2,1)S(1)}, bf16[2,96,768]{2,1,0:T(8,128)(2,1)S(1)}, u32[]{:S(2)}, u32[]{:S(2)}) %collective-permute-start.29) | collective-permute-done | bytes 294944 | tf_op jit(solution)/shard_map/ppermute | solution.py:83
  48.3 8.0 %collective-permute-done.25 = bf16[2,2,24,3840]{3,2,1,0:T(8,128)(2,1)S(1)} collective-permute-done((bf16[2,2,24,3840]{3,2,1,0:T(8,128)(2,1)S(1)}, bf16[2,2,24,3840]{3,2,1,0:T(8,128)(2,1)S(1)}, u32[]{:S(2)}, u32[]{:S(2)}) %collective-permute-start.25) | collective-permute-done | bytes 737312 | tf_op jit(solution)/shard_map/ppermute | solution.py:83
  63.8 35.8 %collective-permute-done.7 = bf16[2,2,24,1280]{3,2,1,0:T(8,128)(2,1)S(1)} collective-permute-done((bf16[2,2,24,1280]{3,2,1,0:T(8,128)(2,1)S(1)}, bf16[2,2,24,1280]{3,2,1,0:T(8,128)(2,1)S(1)}, u32[]{:S(2)}, u32[]{:S(2)}) %collective-permute-start.7) | collective-permute-done | bytes 245792 | tf_op jit(solution)/shard_map/ppermute | solution.py:83
  103.2 5.4 %collective-permute-done.8 = bf16[2,2,2,24,1280]{4,3,2,1,0:T(8,128)(2,1)S(1)} collective-permute-done((bf16[2,2,2,24,1280]{4,3,2,1,0:T(8,128)(2,1)S(1)}, bf16[2,2,2,24,1280]{4,3,2,1,0:T(8,128)(2,1)S(1)}, u32[]{:S(2)}, u32[]{:S(2)}) %collective-permute-start.8) | collective-permute-done | bytes 491552 | tf_op jit(solution)/shard_map/ppermute | solution.py:83
  119.9 5.0 %project.1 = (bf16[256,768]{1,0:T(8,128)(2,1)}, f32[8,768]{1,0:T(8,128)}, bf16[192,256]{1,0:T(8,128)(2,1)}, bf16[192,256]{1,0:T(8,128)(2,1)}, bf16[192,256]{1,0:...) custom-call(s32[7]{0:T(128)} %pad_add_fusion.where_ref, ...), custom_call_target="tpu_custom_call" | custom-call | flops 905969664 | bytes 7077888 | tf_op jit(solution)/shard_map/project/pallas_call | solution.py:384
  134.8 5.9 %collective-permute-done.11.refs_2_ = bf16[192,256]{1,0:T(8,128)(2,1)S(1)} collective-permute-done((bf16[192,256]{1,0:T(8,128)(2,1)}, bf16[192,256]{1,0:T(8,128)(2,1)S(1)}, u32[]{:S(2)}, u32[]{:S(2)}) %collective-permute-start.11) | collective-permute-done | bytes 98336 | tf_op jit(solution)/shard_map/ppermute | solution.py:605
  140.8 3.5 collective-permute-start.15
  147.0 6.4 %collective-permute-done.14.refs_6_ = bf16[384,256]{1,0:T(8,128)(2,1)} collective-permute-done((bf16[384,256]{1,0:T(8,128)(2,1)}, bf16[384,256]{1,0:T(8,128)(2,1)}, u32[]{:S(2)}, u32[]{:S(2)}) %collective-permute-start.14) | collective-permute-done | bytes 196640 | tf_op jit(solution)/shard_map/ppermute | solution.py:605
  161.2 4.3 %collective-permute-done.18.refs_10_ = bf16[384,256]{1,0:T(8,128)(2,1)} collective-permute-done((bf16[384,256]{1,0:T(8,128)(2,1)}, bf16[384,256]{1,0:T(8,128)(2,1)}, u32[]{:S(2)}, u32[]{:S(2)}) %collective-permute-start.18) | collective-permute-done | bytes 196640 | tf_op jit(solution)/shard_map/ppermute | solution.py:631
  167.9 15.9 %attend.1 = (bf16[4,576,256]{2,1,0:T(8,128)(2,1)}, bf16[4,384,256]{2,1,0:T(8,128)(2,1)}, f32[4,192,256]{2,1,0:T(8,128)}, f32[4,8,256]{2,1,0:T(8,128)}, bf16[192,...) custom-call(s32[7]{0:T(128)} %pad_add_fusion.where_ref, ...), custom_call_target="tpu_custom_call" | custom-call | flops 805306368 | bytes 4718592 | tf_op jit(solution)/shard_map/attend/pallas_call | solution.py:315
  183.8 5.8 %collective-permute-start.20 = (bf16[192,256]{1,0:T(8,128)(2,1)}, bf16[192,256]{1,0:T(8,128)(2,1)S(1)}, u32[]{:S(2)}, u32[]{:S(2)}) collective-permute-start(bf16[192,256]{1,0:T(8,128)(2,1)} %get-tuple-element.66), channel_id=1, source_target_pairs={{0,24},{4,28},{8,0},{12,4},{16,8},{20,12},{24,16},{28,20},{1,25},{... | collective-permute-start | bytes 294920 | tf_op jit(solution)/shard_map/ppermute | solution.py:605
  194.3 4.8 %bitcast_select_fusion.refs_4_.refs_6_ = bf16[768,3840]{1,0:T(8,128)(2,1)} fusion(pred[768]{0:T(1024)(128)(4,1)S(1)} %iota.146, bf16[2,2,2,2,24,3840]{5,4,3,2,1,0:T(8,128)(2,1)} %collective-permute-done.27, bf16[2,2,2,2,24,3840]{5,4,3,2,1,0:T(8,128)(2,1)S(1)} %broadcast_select_fusion), kind=kLoop, calls=%fused_computation.1 | loop fusion | flops 2949120 | bytes 11797248 | tf_op jit(solution)/shard_map/jit(_where)/select_n | solution.py:98
  199.8 13.6 %middle.1 = (f32[256,768]{1,0:T(8,128)}, bf16[768,256]{1,0:T(8,128)(2,1)}, bf16[256,768]{1,0:T(8,128)(2,1)}, bf16[256,768]{1,0:T(8,128)(2,1)}, f32[256,768]{1,0:...) custom-call(s32[7]{0:T(128)} %pad_add_fusion.where_ref, ...), custom_call_target="tpu_custom_call" | custom-call | flops 5435817984 | bytes 17301504 | tf_op jit(solution)/shard_map/middle/pallas_call | solution.py:484
  237.0 20.7 %attend_back.1 = (bf16[192,256]{1,0:T(8,128)(2,1)}, bf16[192,256]{1,0:T(8,128)(2,1)}, bf16[192,256]{1,0:T(8,128)(2,1)}, bf16[192,256]{1,0:T(8,128)(2,1)}, bf16[3...) custom-call(s32[7]{0:T(128)} %pad_add_fusion.where_ref, ...), custom_call_target="tpu_custom_call" | custom-call | flops 2013265920 | bytes 6291456 | tf_op jit(solution)/shard_map/attend_back/pallas_call | solution.py:338
  257.7 3.7 collective-permute-start.36
  265.4 5.5 %collective-permute-done.37 = bf16[192,256]{1,0:T(8,128)(2,1)S(1)} collective-permute-done((bf16[192,256]{1,0:T(8,128)(2,1)}, bf16[192,256]{1,0:T(8,128)(2,1)S(1)}, u32[]{:S(2)}, u32[]{:S(2)}) %collective-permute-start.37) | collective-permute-done | bytes 98336 | tf_op jit(solution)/shard_map/ppermute | solution.py:605
  274.9 4.0 collective-permute-done.42
  282.5 3.4 collective-permute-start.41
  286.9 4.3 %collective-permute-done.41 = bf16[384,256]{1,0:T(8,128)(2,1)S(1)} collective-permute-done((bf16[384,256]{1,0:T(8,128)(2,1)S(1)}, bf16[384,256]{1,0:T(8,128)(2,1)S(1)}, u32[]{:S(2)}, u32[]{:S(2)}) %collective-permute-start.41) | collective-permute-done | bytes 196640 | tf_op jit(solution)/shard_map/ppermute | solution.py:605
  291.2 11.0 %collective-permute-done.43 = bf16[384,256]{1,0:T(8,128)(2,1)S(1)} collective-permute-done((bf16[384,256]{1,0:T(8,128)(2,1)S(1)}, bf16[384,256]{1,0:T(8,128)(2,1)S(1)}, u32[]{:S(2)}, u32[]{:S(2)}) %collective-permute-start.43) | collective-permute-done | bytes 196640 | tf_op jit(solution)/shard_map/ppermute | solution.py:605
  319.6 10.7 %collective-permute-done.52 = bf16[192,1152]{1,0:T(8,128)(2,1)S(1)} collective-permute-done((bf16[192,1152]{1,0:T(8,128)(2,1)S(1)}, bf16[192,1152]{1,0:T(8,128)(2,1)S(1)}, u32[]{:S(2)}, u32[]{:S(2)}) %collective-permute-start.52) | collective-permute-done | bytes 442400 | tf_op jit(solution)/shard_map/ppermute | solution.py:83
  333.7 4.0 collective-permute-done.53
  364.3 14.5 %collective-permute-done.62 = bf16[2,2,2,96,768]{4,3,0,1,2:T(8,128)(2,1)S(1)} collective-permute-done((bf16[2,2,2,96,768]{4,3,0,1,2:T(8,128)(2,1)}, bf16[2,2,2,96,768]{4,3,0,1,2:T(8,128)(2,1)S(1)}, u32[]{:S(2)}, u32[]{:S(2)}) %collective-permute-start.62) | collective-permute-done | bytes 1179680 | tf_op jit(solution)/shard_map/ppermute | solution.py:83
  380.0 15.2 %collective-permute-done.57 = bf16[192,3840]{1,0:T(8,128)(2,1)} collective-permute-done((bf16[192,3840]{1,0:T(8,128)(2,1)}, bf16[192,3840]{1,0:T(8,128)(2,1)}, u32[]{:S(2)}, u32[]{:S(2)}) %collective-permute-start.57) | collective-permute-done | bytes 1474592 | tf_op jit(solution)/shard_map/ppermute | solution.py:83
  398.8 5.4 %collective-permute-done.63 = bf16[2,2,96,768]{3,2,0,1:T(8,128)(2,1)S(1)} collective-permute-done((bf16[2,2,96,768]{3,2,0,1:T(8,128)(2,1)S(1)}, bf16[2,2,96,768]{3,2,0,1:T(8,128)(2,1)S(1)}, u32[]{:S(2)}, u32[]{:S(2)}) %collective-permute-start.63) | collective-permute-done | bytes 589856 | tf_op jit(solution)/shard_map/ppermute | solution.py:83
  404.6 4.0 collective-permute-done.58
  408.9 6.8 %collective-permute-done.64 = bf16[2,96,768]{2,1,0:T(8,128)(2,1)S(1)} collective-permute-done((bf16[2,96,768]{2,1,0:T(8,128)(2,1)S(1)}, bf16[2,96,768]{2,1,0:T(8,128)(2,1)S(1)}, u32[]{:S(2)}, u32[]{:S(2)}) %collective-permute-start.64) | collective-permute-done | bytes 294944 | tf_op jit(solution)/shard_map/ppermute | solution.py:83
  415.9 4.3 collective-permute-done.59
  423.1 4.6 %collective-permute-done.65 = bf16[96,768]{1,0:T(8,128)(2,1)S(1)} collective-permute-done((bf16[96,768]{1,0:T(8,128)(2,1)S(1)}, bf16[96,768]{1,0:T(8,128)(2,1)S(1)}, u32[]{:S(2)}, u32[]{:S(2)}) %collective-permute-start.65) | collective-permute-done | bytes 147488 | tf_op jit(solution)/shard_map/ppermute | solution.py:83
  (364 shorter events, 159.3 us)
Async XLA Ops:
  2.4 21.8 %collective-permute-start.23 = (bf16[24,3840]{1,0:T(8,128)(2,1)S(1)}, bf16[24,3840]{1,0:T(8,128)(2,1)S(1)}, u32[]{:S(2)}, u32[]{:S(2)}) collective-permute-start(bf16[24,3840]{1,0:T(8,128)(2,1)S(1)} %constant_dynamic-update-slice_fusion), channel_id=1, source_target_pairs={{0,16},{4,20},{8,24},{12,28},{16,0},{20,4},{24,8},{28,12},{1,17},{... | collective-permute-start | bytes 552968 | tf_op jit(solution)/shard_map/ppermute | solution.py:83
  9.1 17.3 %collective-permute-start.5 = (bf16[24,1280]{1,0:T(8,128)(2,1)S(1)}, bf16[24,1280]{1,0:T(8,128)(2,1)S(1)}, u32[]{:S(2)}, u32[]{:S(2)}) collective-permute-start(bf16[24,1280]{1,0:T(8,128)(2,1)S(1)} %fusion.59), channel_id=1, source_target_pairs={{0,16},{4,20},{8,24},{12,28},{16,0},{20,4},{24,8},{28,12},{1,17},{... | collective-permute-start | bytes 184328 | tf_op jit(solution)/shard_map/ppermute | solution.py:83
  9.2 14.9 %collective-permute-start = (bf16[24,1152]{1,0:T(8,128)(2,1)S(1)}, bf16[24,1152]{1,0:T(8,128)(2,1)S(1)}, u32[]{:S(2)}, u32[]{:S(2)}) collective-permute-start(bf16[24,1152]{1,0:T(8,128)(2,1)S(1)} %get-tuple-element.148), channel_id=1, source_target_pairs={{0,16},{4,20},{8,24},{12,28},{16,0},{20,4},{24,8},{28,12},{1,17},{... | collective-permute-start | bytes 165896 | tf_op jit(solution)/shard_map/ppermute | solution.py:83
  12.1 27.6 %collective-permute-start.28 = (bf16[96,768]{1,0:T(8,128)(2,1)}, bf16[96,768]{1,0:T(8,128)(2,1)S(1)}, u32[]{:S(2)}, u32[]{:S(2)}) collective-permute-start(bf16[96,768]{1,0:T(8,128)(2,1)} %param.30), channel_id=1, source_target_pairs={{0,16},{4,20},{8,24},{12,28},{16,0},{20,4},{24,8},{28,12},{1,17},{... | collective-permute-start | bytes 442376 | tf_op jit(solution)/shard_map/ppermute | solution.py:83
  24.1 16.0 %collective-permute-start.1 = (bf16[2,24,1152]{2,1,0:T(8,128)(2,1)S(1)}, bf16[2,24,1152]{2,1,0:T(8,128)(2,1)S(1)}, u32[]{:S(2)}, u32[]{:S(2)}) collective-permute-start(bf16[2,24,1152]{2,1,0:T(8,128)(2,1)S(1)} %broadcast_select_fusion.15), channel_id=1, source_target_pairs={{0,8},{4,12},{8,0},{12,4},{16,24},{20,28},{24,16},{28,20},{1,9},{5... | collective-permute-start | bytes 331784 | tf_op jit(solution)/shard_map/ppermute | solution.py:83
  24.3 13.6 %collective-permute-start.24 = (bf16[2,24,3840]{2,1,0:T(8,128)(2,1)S(1)}, bf16[2,24,3840]{2,1,0:T(8,128)(2,1)S(1)}, u32[]{:S(2)}, u32[]{:S(2)}) collective-permute-start(bf16[2,24,3840]{2,1,0:T(8,128)(2,1)S(1)} %broadcast_select_fusion.10), channel_id=1, source_target_pairs={{0,8},{4,12},{8,0},{12,4},{16,24},{20,28},{24,16},{28,20},{1,9},{5... | collective-permute-start | bytes 1105928 | tf_op jit(solution)/shard_map/ppermute | solution.py:83
  26.5 31.4 %collective-permute-start.6 = (bf16[2,24,1280]{2,1,0:T(8,128)(2,1)S(1)}, bf16[2,24,1280]{2,1,0:T(8,128)(2,1)S(1)}, u32[]{:S(2)}, u32[]{:S(2)}) collective-permute-start(bf16[2,24,1280]{2,1,0:T(8,128)(2,1)S(1)} %broadcast_select_fusion.14), channel_id=1, source_target_pairs={{0,8},{4,12},{8,0},{12,4},{16,24},{20,28},{24,16},{28,20},{1,9},{5... | collective-permute-start | bytes 368648 | tf_op jit(solution)/shard_map/ppermute | solution.py:83
  38.1 18.2 %collective-permute-start.25 = (bf16[2,2,24,3840]{3,2,1,0:T(8,128)(2,1)S(1)}, bf16[2,2,24,3840]{3,2,1,0:T(8,128)(2,1)S(1)}, u32[]{:S(2)}, u32[]{:S(2)}) collective-permute-start(bf16[2,2,24,3840]{3,2,1,0:T(8,128)(2,1)S(1)} %broadcast_select_fusion.6), channel_id=1, source_target_pairs={{0,4},{4,0},{8,12},{12,8},{16,20},{20,16},{24,28},{28,24},{1,5},{5... | collective-permute-start | bytes 2211848 | tf_op jit(solution)/shard_map/ppermute | solution.py:83
  40.3 18.5 %collective-permute-start.2 = (bf16[2,2,24,1152]{3,2,1,0:T(8,128)(2,1)S(1)}, bf16[2,2,24,1152]{3,2,1,0:T(8,128)(2,1)S(1)}, u32[]{:S(2)}, u32[]{:S(2)}) collective-permute-start(bf16[2,2,24,1152]{3,2,1,0:T(8,128)(2,1)S(1)} %broadcast_select_fusion.13), channel_id=1, source_target_pairs={{0,4},{4,0},{8,12},{12,8},{16,20},{20,16},{24,28},{28,24},{1,5},{5... | collective-permute-start | bytes 663560 | tf_op jit(solution)/shard_map/ppermute | solution.py:83
  46.7 16.0 %collective-permute-start.30 = (bf16[2,2,96,768]{3,2,1,0:T(8,128)(2,1)S(1)}, bf16[2,2,96,768]{3,2,1,0:T(8,128)(2,1)S(1)}, u32[]{:S(2)}, u32[]{:S(2)}) collective-permute-start(bf16[2,2,96,768]{3,2,1,0:T(8,128)(2,1)S(1)} %broadcast_select_fusion.7), channel_id=1, source_target_pairs={{0,2},{1,3},{2,0},{3,1},{4,6},{5,7},{6,4},{7,5},{8,10},{9,11},{10,... | collective-permute-start | bytes 1769480 | tf_op jit(solution)/shard_map/ppermute | solution.py:83
  56.5 44.1 %collective-permute-start.26 = (bf16[2,2,2,24,3840]{4,3,2,1,0:T(8,128)(2,1)S(1)}, bf16[2,2,2,24,3840]{4,3,2,1,0:T(8,128)(2,1)S(1)}, u32[]{:S(2)}, u32[]{:S(2)}) collective-permute-start(bf16[2,2,2,24,3840]{4,3,2,1,0:T(8,128)(2,1)S(1)} %broadcast_select_fusion.2), channel_id=1, source_target_pairs={{0,2},{1,3},{2,0},{3,1},{4,6},{5,7},{6,4},{7,5},{8,10},{9,11},{10,... | collective-permute-start | bytes 4423688 | tf_op jit(solution)/shard_map/ppermute | solution.py:83
  58.0 41.6 %collective-permute-start.7 = (bf16[2,2,24,1280]{3,2,1,0:T(8,128)(2,1)S(1)}, bf16[2,2,24,1280]{3,2,1,0:T(8,128)(2,1)S(1)}, u32[]{:S(2)}, u32[]{:S(2)}) collective-permute-start(bf16[2,2,24,1280]{3,2,1,0:T(8,128)(2,1)S(1)} %broadcast_select_fusion.12), channel_id=1, source_target_pairs={{0,2},{1,3},{2,0},{3,1},{4,6},{5,7},{6,4},{7,5},{8,10},{9,11},{10,... | collective-permute-start | bytes 737288 | tf_op jit(solution)/shard_map/ppermute | solution.py:83
  58.9 50.8 %collective-permute-start.3 = (bf16[2,2,2,24,1152]{4,3,2,1,0:T(8,128)(2,1)S(1)}, bf16[2,2,2,24,1152]{4,3,2,1,0:T(8,128)(2,1)S(1)}, u32[]{:S(2)}, u32[]{:S(2)}) collective-permute-start(bf16[2,2,2,24,1152]{4,3,2,1,0:T(8,128)(2,1)S(1)} %broadcast_select_fusion.9), channel_id=1, source_target_pairs={{0,2},{1,3},{2,0},{3,1},{4,6},{5,7},{6,4},{7,5},{8,10},{9,11},{10,... | collective-permute-start | bytes 1327112 | tf_op jit(solution)/shard_map/ppermute | solution.py:83
  62.9 38.0 %collective-permute-start.31 = (bf16[2,2,2,96,768]{4,3,2,1,0:T(8,128)(2,1)S(1)}, bf16[2,2,2,96,768]{4,3,2,1,0:T(8,128)(2,1)S(1)}, u32[]{:S(2)}, u32[]{:S(2)}) collective-permute-start(bf16[2,2,2,96,768]{4,3,2,1,0:T(8,128)(2,1)S(1)} %broadcast_select_fusion.3), channel_id=1, source_target_pairs={{0,4},{4,0},{8,12},{12,8},{16,20},{20,16},{24,28},{28,24},{1,5},{5... | collective-permute-start | bytes 3538952 | tf_op jit(solution)/shard_map/ppermute | solution.py:83
  100.8 93.4 %collective-permute-start.27 = (bf16[2,2,2,2,24,3840]{5,4,3,2,1,0:T(8,128)(2,1)S(1)}, bf16[2,2,2,2,24,3840]{5,4,3,2,1,0:T(8,128)(2,1)}, u32[]{:S(2)}, u32[]{:S(2)}) collective-permute-start(bf16[2,2,2,2,24,3840]{5,4,3,2,1,0:T(8,128)(2,1)S(1)} %broadcast_select_fusion), channel_id=1, source_target_pairs={{0,1},{1,0},{2,3},{3,2},{4,5},{5,4},{6,7},{7,6},{8,9},{9,8},{10,11... | collective-permute-start | bytes 8847368 | tf_op jit(solution)/shard_map/ppermute | solution.py:83
  102.7 96.4 %collective-permute-start.32 = (bf16[2,2,2,2,96,768]{5,4,3,2,1,0:T(8,128)(2,1)}, bf16[2,2,2,2,96,768]{5,4,3,2,1,0:T(8,128)(2,1)}, u32[]{:S(2)}, u32[]{:S(2)}) collective-permute-start(bf16[2,2,2,2,96,768]{5,4,3,2,1,0:T(8,128)(2,1)} %broadcast_select_fusion.1), channel_id=1, source_target_pairs={{0,1},{1,0},{2,3},{3,2},{4,5},{5,4},{6,7},{7,6},{8,9},{9,8},{10,11... | collective-permute-start | bytes 7077896 | tf_op jit(solution)/shard_map/ppermute | solution.py:83
  125.0 19.3 %collective-permute-start.13 = (bf16[384,256]{1,0:T(8,128)(2,1)}, bf16[384,256]{1,0:T(8,128)(2,1)S(1)}, u32[]{:S(2)}, u32[]{:S(2)}) collective-permute-start(bf16[384,256]{1,0:T(8,128)(2,1)} %get-tuple-element.62), channel_id=1, source_target_pairs={{0,8},{4,12},{8,16},{12,20},{16,24},{20,28},{24,0},{28,4},{1,9},{5... | collective-permute-start | bytes 589832 | tf_op jit(solution)/shard_map/ppermute | solution.py:605
  128.2 12.6 %collective-permute-start.11 = (bf16[192,256]{1,0:T(8,128)(2,1)}, bf16[192,256]{1,0:T(8,128)(2,1)S(1)}, u32[]{:S(2)}, u32[]{:S(2)}) collective-permute-start(bf16[192,256]{1,0:T(8,128)(2,1)} %get-tuple-element.59), channel_id=1, source_target_pairs={{0,16},{4,20},{8,24},{12,28},{16,0},{20,4},{24,8},{28,12},{1,17},{... | collective-permute-start | bytes 294920 | tf_op jit(solution)/shard_map/ppermute | solution.py:605
  140.7 12.7 %collective-permute-start.14 = (bf16[384,256]{1,0:T(8,128)(2,1)}, bf16[384,256]{1,0:T(8,128)(2,1)}, u32[]{:S(2)}, u32[]{:S(2)}) collective-permute-start(bf16[384,256]{1,0:T(8,128)(2,1)} %get-tuple-element.63), channel_id=1, source_target_pairs={{0,16},{4,20},{8,24},{12,28},{16,0},{20,4},{24,8},{28,12},{1,17},{... | collective-permute-start | bytes 589832 | tf_op jit(solution)/shard_map/ppermute | solution.py:605
  140.8 13.2 %collective-permute-start.15 = (bf16[384,256]{1,0:T(8,128)(2,1)}, bf16[384,256]{1,0:T(8,128)(2,1)}, u32[]{:S(2)}, u32[]{:S(2)}) collective-permute-start(bf16[384,256]{1,0:T(8,128)(2,1)} %get-tuple-element.64), channel_id=1, source_target_pairs={{0,24},{4,28},{8,0},{12,4},{16,8},{20,12},{24,16},{28,20},{1,25},{... | collective-permute-start | bytes 589832 | tf_op jit(solution)/shard_map/ppermute | solution.py:605
  183.8 15.2 %collective-permute-start.20 = (bf16[192,256]{1,0:T(8,128)(2,1)}, bf16[192,256]{1,0:T(8,128)(2,1)S(1)}, u32[]{:S(2)}, u32[]{:S(2)}) collective-permute-start(bf16[192,256]{1,0:T(8,128)(2,1)} %get-tuple-element.66), channel_id=1, source_target_pairs={{0,24},{4,28},{8,0},{12,4},{16,8},{20,12},{24,16},{28,20},{1,25},{... | collective-permute-start | bytes 294920 | tf_op jit(solution)/shard_map/ppermute | solution.py:605
  225.0 122.9 %collective-permute-start.61 = (bf16[2,2,2,2,96,768]{5,4,0,1,3,2:T(8,128)(2,1)}, bf16[2,2,2,2,96,768]{5,4,0,1,3,2:T(8,128)(2,1)}, u32[]{:S(2)}, u32[]{:S(2)}) collective-permute-start(bf16[2,2,2,2,96,768]{5,4,0,1,3,2:T(8,128)(2,1)} %select_bitcast_fusion), channel_id=1, source_target_pairs={{0,1},{1,0},{2,3},{3,2},{4,5},{5,4},{6,7},{7,6},{8,9},{9,8},{10,11... | collective-permute-start | bytes 7077896 | tf_op jit(solution)/shard_map/ppermute | solution.py:83
  274.9 78.8 %collective-permute-start.56 = (bf16[384,3840]{1,0:T(8,128)(2,1)}, bf16[384,3840]{1,0:T(8,128)(2,1)}, u32[]{:S(2)}, u32[]{:S(2)}) collective-permute-start(bf16[384,3840]{1,0:T(8,128)(2,1)} %pad_maximum_fusion), channel_id=1, source_target_pairs={{0,1},{1,0},{2,3},{3,2},{4,5},{5,4},{6,7},{7,6},{8,9},{9,8},{10,11... | collective-permute-start | bytes 8847368 | tf_op jit(solution)/shard_map/ppermute | solution.py:83
  285.9 16.4 %collective-permute-start.43 = (bf16[384,256]{1,0:T(8,128)(2,1)S(1)}, bf16[384,256]{1,0:T(8,128)(2,1)S(1)}, u32[]{:S(2)}, u32[]{:S(2)}) collective-permute-start(bf16[384,256]{1,0:T(8,128)(2,1)S(1)} %get-tuple-element.131), channel_id=1, source_target_pairs={{0,16},{4,20},{8,24},{12,28},{16,0},{20,4},{24,8},{28,12},{1,17},{... | collective-permute-start | bytes 589832 | tf_op jit(solution)/shard_map/ppermute | solution.py:605
  286.6 15.7 %collective-permute-start.45 = (bf16[384,256]{1,0:T(8,128)(2,1)S(1)}, bf16[384,256]{1,0:T(8,128)(2,1)S(1)}, u32[]{:S(2)}, u32[]{:S(2)}) collective-permute-start(bf16[384,256]{1,0:T(8,128)(2,1)S(1)} %get-tuple-element.130), channel_id=1, source_target_pairs={{0,8},{4,12},{8,16},{12,20},{16,24},{20,28},{24,0},{28,4},{1,9},{5... | collective-permute-start | bytes 589832 | tf_op jit(solution)/shard_map/ppermute | solution.py:605
  317.7 12.6 %collective-permute-start.52 = (bf16[192,1152]{1,0:T(8,128)(2,1)S(1)}, bf16[192,1152]{1,0:T(8,128)(2,1)S(1)}, u32[]{:S(2)}, u32[]{:S(2)}) collective-permute-start(bf16[192,1152]{1,0:T(8,128)(2,1)S(1)} %slice.395), channel_id=1, source_target_pairs={{0,2},{1,3},{2,0},{3,1},{4,6},{5,7},{6,4},{7,5},{8,10},{9,11},{10,... | collective-permute-start | bytes 1327112 | tf_op jit(solution)/shard_map/ppermute | solution.py:83
  319.5 13.6 %collective-permute-start.47 = (bf16[192,1280]{1,0:T(8,128)(2,1)S(1)}, bf16[192,1280]{1,0:T(8,128)(2,1)S(1)}, u32[]{:S(2)}, u32[]{:S(2)}) collective-permute-start(bf16[192,1280]{1,0:T(8,128)(2,1)S(1)} %slice.383), channel_id=1, source_target_pairs={{0,4},{4,0},{8,12},{12,8},{16,20},{20,16},{24,28},{28,24},{1,5},{5... | collective-permute-start | bytes 1474568 | tf_op jit(solution)/shard_map/ppermute | solution.py:83
  343.8 16.5 %collective-permute-start.55 = (bf16[24,1152]{1,0:T(8,128)(2,1)S(1)}, bf16[24,1152]{1,0:T(8,128)(2,1)S(1)}, u32[]{:S(2)}, u32[]{:S(2)}) collective-permute-start(bf16[24,1152]{1,0:T(8,128)(2,1)S(1)} %slice.401), channel_id=1, source_target_pairs={{0,16},{4,20},{8,24},{12,28},{16,0},{20,4},{24,8},{28,12},{1,17},{... | collective-permute-start | bytes 165896 | tf_op jit(solution)/shard_map/ppermute | solution.py:83
  346.1 14.9 %collective-permute-start.50 = (bf16[24,1280]{1,0:T(8,128)(2,1)S(1)}, bf16[24,1280]{1,0:T(8,128)(2,1)S(1)}, u32[]{:S(2)}, u32[]{:S(2)}) collective-permute-start(bf16[24,1280]{1,0:T(8,128)(2,1)S(1)} %slice.389), channel_id=1, source_target_pairs={{0,16},{4,20},{8,24},{12,28},{16,0},{20,4},{24,8},{28,12},{1,17},{... | collective-permute-start | bytes 184328 | tf_op jit(solution)/shard_map/ppermute | solution.py:83
  353.3 25.6 %collective-permute-start.62 = (bf16[2,2,2,96,768]{4,3,0,1,2:T(8,128)(2,1)}, bf16[2,2,2,96,768]{4,3,0,1,2:T(8,128)(2,1)S(1)}, u32[]{:S(2)}, u32[]{:S(2)}) collective-permute-start(bf16[2,2,2,96,768]{4,3,0,1,2:T(8,128)(2,1)} %select_bitcast_fusion.1), channel_id=1, source_target_pairs={{0,4},{4,0},{8,12},{12,8},{16,20},{20,16},{24,28},{28,24},{1,5},{5... | collective-permute-start | bytes 3538952 | tf_op jit(solution)/shard_map/ppermute | solution.py:83
  359.7 35.5 %collective-permute-start.57 = (bf16[192,3840]{1,0:T(8,128)(2,1)}, bf16[192,3840]{1,0:T(8,128)(2,1)}, u32[]{:S(2)}, u32[]{:S(2)}) collective-permute-start(bf16[192,3840]{1,0:T(8,128)(2,1)} %slice.410), channel_id=1, source_target_pairs={{0,2},{1,3},{2,0},{3,1},{4,6},{5,7},{6,4},{7,5},{8,10},{9,11},{10,... | collective-permute-start | bytes 4423688 | tf_op jit(solution)/shard_map/ppermute | solution.py:83
  379.4 24.8 %collective-permute-start.63 = (bf16[2,2,96,768]{3,2,0,1:T(8,128)(2,1)S(1)}, bf16[2,2,96,768]{3,2,0,1:T(8,128)(2,1)S(1)}, u32[]{:S(2)}, u32[]{:S(2)}) collective-permute-start(bf16[2,2,96,768]{3,2,0,1:T(8,128)(2,1)S(1)} %select_bitcast_fusion.2), channel_id=1, source_target_pairs={{0,2},{1,3},{2,0},{3,1},{4,6},{5,7},{6,4},{7,5},{8,10},{9,11},{10,... | collective-permute-start | bytes 1769480 | tf_op jit(solution)/shard_map/ppermute | solution.py:83
  (91 other events, 807.2 us)
where the time goes:
time: 432 us; the launch traced here: 431 us
  waiting for transfers between devices  217 us (50%)
  starting transfers between devices  68.7 us (16%)
  Pallas kernels  55.2 us (13%)
  other arithmetic  42.2 us (10%)
  local copies, waits for them, and re-layouts  26.6 us (6%)
  matrix products  19.1 us (4%)
    ppermute x40, waiting for transfers between devices, exchange(): return lax.ppermute(value, axis, [(i, i ^ bit) for i in range(sizes[axis])])  160 us
    ppermute x18, waiting for transfers between devices, shift_far(): lax.ppermute(value, 'seq', [(i, (i + 2 * shift) % seq) for i in range(seq)])  40.6 us
    ppermute x40, starting transfers between devices, exchange(): return lax.ppermute(value, axis, [(i, i ^ bit) for i in range(sizes[axis])])  32.2 us
    ppermute x18, starting transfers between devices, shift_far(): lax.ppermute(value, 'seq', [(i, (i + 2 * shift) % seq) for i in range(seq)])  30.3 us
    pallas_call x1, Pallas kernels, attend_back(): pl.pallas_call(functools.partial(backward_kernel, heads, dim, far), name=...  20.7 us
    select_n x20, other arithmetic, gather(): value = jnp.where(side == own_bit(step), mine, other)  19.9 us
    dot_general x15, matrix products, dot(): lax.dot_general(left, right, (((left_dim,), (right_dim,)), ((), ())), pre...  19.1 us
    ppermute x8, waiting for transfers between devices, to_pair(): return lax.ppermute(value, 'seq', [(i, i ^ 1) for i in range(seq)])  16.9 us
  transfers between devices with their start and end apart: 66, of which 35 were waited for; matrix products, arithmetic and copies ran while one was open for 16% of the time, Pallas kernels for 10%

commit v1 on v0

--- a/solution.py
+++ b/solution.py
@@ -87,9 +87,11 @@
     place = {step: n for n, step in enumerate(bits_of(sizes))}
     have, value = [], shard
     for n, step in enumerate(steps):
+        if n == len(steps) - 1 and not join:
+            value = lax.optimization_barrier(value.reshape((-1,) + shard.shape))
         other = exchange(value, step, sizes)
         if n == len(steps) - 1 and not join:
-            return (value.reshape((-1,) + shard.shape), other.reshape((-1,) + shard.shape))
+            return (value, other)
         at = sum(1 for m in have if m < place[step])
         have.append(place[step])
         mine, other = jnp.expand_dims(value, at), jnp.expand_dims(other, at)
@@ -581,7 +583,9 @@
 
     qkv_one = gather(w_qkv[:, :half], order_one, sizes)
     qkv_two = gather(jnp.concatenate([w_qkv[:, half:], small], axis=1), order_two, sizes)
-    fc_proj_full = gather(jnp.concatenate([w_fc, w_attn_out], axis=1), order_one, sizes)
+    fc_proj_full = lax.optimization_barrier(
+        gather(jnp.concatenate([w_fc, w_attn_out], axis=1), order_one, sizes)
+    )
     out_aligned = w_mlp_out.shape[0] % 32 == 0
     out_full = gather(w_mlp_out, order_two, sizes, join=not out_aligned)
     if not out_aligned:
@@ -690,7 +694,8 @@
         ],
         axis=0,
     )
-    sorted_two = dot(attn_in, sort_two, 1, 0).astype(bf16)
+    late_attn, _ = lax.optimization_barrier((attn_in, back_slots[0]))
+    sorted_two = dot(late_attn, sort_two, 1, 0).astype(bf16)
     g_qkv_one = [
         dot(sorted_one[:, low : low + part], qkv_grad_t[:half], 0, 1).astype(bf16)
         for low in (0, part)

time: 432 us -> 448 us (1.037)
  waiting for transfers between devices: 217 us -> 232 us
  starting transfers between devices: 68.7 us -> 76.3 us
    ppermute x40, waiting for transfers between devices: 160 us -> 175 us  [exchange(): return lax.ppermute(value, axis, [(i, i ^ bit) for i in range(sizes[axis])])]
    ppermute x40, starting transfers between devices: 32.2 us -> 37.9 us  [exchange(): return lax.ppermute(value, axis, [(i, i ^ bit) for i in range(sizes[axis])])]
    select_n x20 -> x19, other arithmetic: 19.9 us -> 16.6 us  [gather(): value = jnp.where(side == own_bit(step), mine, other)]
    unnamed x122 -> x104, local copies, waits for them, and re-layouts: 9.8 us -> 8.15 us
  transfers between devices with their start and end apart: 66 -> 66, of which waited for: 35 -> 35; matrix products, arithmetic and copies ran while one was open for 16% -> 14% of each run, Pallas kernels for 10% -> 9%
where the time goes in v1:
time: 448 us; the launch traced here: 447 us
  waiting for transfers between devices  232 us (52%)
  starting transfers between devices  76.3 us (17%)
  Pallas kernels  55.2 us (12%)
  other arithmetic  39 us (9%)
  local copies, waits for them, and re-layouts  24.4 us (5%)
  matrix products  18.5 us (4%)
    ppermute x40, waiting for transfers between devices, exchange(): return lax.ppermute(value, axis, [(i, i ^ bit) for i in range(sizes[axis])])  175 us
    ppermute x18, waiting for transfers between devices, shift_far(): lax.ppermute(value, 'seq', [(i, (i + 2 * shift) % seq) for i in range(seq)])  40.4 us
    ppermute x40, starting transfers between devices, exchange(): return lax.ppermute(value, axis, [(i, i ^ bit) for i in range(sizes[axis])])  37.9 us
    ppermute x18, starting transfers between devices, shift_far(): lax.ppermute(value, 'seq', [(i, (i + 2 * shift) % seq) for i in range(seq)])  29.3 us
    pallas_call x1, Pallas kernels, attend_back(): pl.pallas_call(functools.partial(backward_kernel, heads, dim, far), name=...  20.7 us
    dot_general x15, matrix products, dot(): lax.dot_general(left, right, (((left_dim,), (right_dim,)), ((), ())), pre...  18.5 us
    select_n x19, other arithmetic, gather(): value = jnp.where(side == own_bit(step), mine, other)  16.6 us
    ppermute x8, waiting for transfers between devices, to_pair(): return lax.ppermute(value, 'seq', [(i, i ^ 1) for i in range(seq)])  16.3 us
  transfers between devices with their start and end apart: 66, of which 35 were waited for; matrix products, arithmetic and copies ran while one was open for 14% of the time, Pallas kernels for 9%

profile of v1, /device:TPU:0, one launch (start us, length us, event | category | flops | bytes accessed | tf_op | source)
XLA Modules:
  0.0 446.7 jit_solution(12082165503187161272)
XLA Ops:
  2.4 4.1 collective-permute-start.23
  12.4 9.2 %collective-permute-done.23 = bf16[24,3840]{1,0:T(8,128)(2,1)S(1)} collective-permute-done((bf16[24,3840]{1,0:T(8,128)(2,1)S(1)}, bf16[24,3840]{1,0:T(8,128)(2,1)S(1)}, u32[]{:S(2)}, u32[]{:S(2)}) %collective-permute-start.23) | collective-permute-done | bytes 184352 | tf_op jit(solution)/shard_map/ppermute | solution.py:83
  24.3 10.0 %collective-permute-done.24 = bf16[2,24,3840]{2,1,0:T(8,128)(2,1)S(1)} collective-permute-done((bf16[2,24,3840]{2,1,0:T(8,128)(2,1)S(1)}, bf16[2,24,3840]{2,1,0:T(8,128)(2,1)S(1)}, u32[]{:S(2)}, u32[]{:S(2)}) %collective-permute-start.24) | collective-permute-done | bytes 368672 | tf_op jit(solution)/shard_map/ppermute | solution.py:83
  38.5 4.0 collective-permute-done.6
  44.1 8.7 %collective-permute-done.25 = bf16[2,2,24,3840]{3,2,1,0:T(8,128)(2,1)S(1)} collective-permute-done((bf16[2,2,24,3840]{3,2,1,0:T(8,128)(2,1)S(1)}, bf16[2,2,24,3840]{3,2,1,0:T(8,128)(2,1)S(1)}, u32[]{:S(2)}, u32[]{:S(2)}) %collective-permute-start.25) | collective-permute-done | bytes 737312 | tf_op jit(solution)/shard_map/ppermute | solution.py:83
  57.8 41.3 %collective-permute-done.30 = bf16[2,2,96,768]{3,2,1,0:T(8,128)(2,1)S(1)} collective-permute-done((bf16[2,2,96,768]{3,2,1,0:T(8,128)(2,1)S(1)}, bf16[2,2,96,768]{3,2,1,0:T(8,128)(2,1)S(1)}, u32[]{:S(2)}, u32[]{:S(2)}) %collective-permute-start.30) | collective-permute-done | bytes 589856 | tf_op jit(solution)/shard_map/ppermute | solution.py:83
  102.9 22.4 %collective-permute-done.31 = bf16[2,2,2,96,768]{4,3,2,1,0:T(8,128)(2,1)S(1)} collective-permute-done((bf16[2,2,2,96,768]{4,3,2,1,0:T(8,128)(2,1)S(1)}, bf16[2,2,2,96,768]{4,3,2,1,0:T(8,128)(2,1)S(1)}, u32[]{:S(2)}, u32[]{:S(2)}) %collective-permute-start.31) | collective-permute-done | bytes 1179680 | tf_op jit(solution)/shard_map/ppermute | solution.py:83
  140.6 5.0 %project.1 = (bf16[256,768]{1,0:T(8,128)(2,1)}, f32[8,768]{1,0:T(8,128)}, bf16[192,256]{1,0:T(8,128)(2,1)}, bf16[192,256]{1,0:T(8,128)(2,1)}, bf16[192,256]{1,0:...) custom-call(s32[7]{0:T(128)} %pad_add_fusion.where_ref, ...), custom_call_target="tpu_custom_call" | custom-call | flops 905969664 | bytes 7077888 | tf_op jit(solution)/shard_map/project/pallas_call | solution.py:386
  150.0 3.4 collective-permute-done.10.refs_1_
  155.0 5.9 %collective-permute-done.11.refs_2_ = bf16[192,256]{1,0:T(8,128)(2,1)S(1)} collective-permute-done((bf16[192,256]{1,0:T(8,128)(2,1)}, bf16[192,256]{1,0:T(8,128)(2,1)S(1)}, u32[]{:S(2)}, u32[]{:S(2)}) %collective-permute-start.11) | collective-permute-done | bytes 98336 | tf_op jit(solution)/shard_map/ppermute | solution.py:609
  165.5 6.8 %collective-permute-done.14.refs_6_ = bf16[384,256]{1,0:T(8,128)(2,1)} collective-permute-done((bf16[384,256]{1,0:T(8,128)(2,1)}, bf16[384,256]{1,0:T(8,128)(2,1)}, u32[]{:S(2)}, u32[]{:S(2)}) %collective-permute-start.14) | collective-permute-done | bytes 196640 | tf_op jit(solution)/shard_map/ppermute | solution.py:609
  180.1 4.2 collective-permute-done.18.refs_10_
  184.4 3.2 collective-permute-done.19.refs_11_
  187.5 15.9 %attend.1 = (bf16[4,576,256]{2,1,0:T(8,128)(2,1)}, bf16[4,384,256]{2,1,0:T(8,128)(2,1)}, f32[4,192,256]{2,1,0:T(8,128)}, f32[4,8,256]{2,1,0:T(8,128)}, bf16[192,...) custom-call(s32[7]{0:T(128)} %pad_add_fusion.where_ref, ...), custom_call_target="tpu_custom_call" | custom-call | flops 805306368 | bytes 4718592 | tf_op jit(solution)/shard_map/attend/pallas_call | solution.py:317
  203.4 6.4 %collective-permute-start.20 = (bf16[192,256]{1,0:T(8,128)(2,1)}, bf16[192,256]{1,0:T(8,128)(2,1)S(1)}, u32[]{:S(2)}, u32[]{:S(2)}) collective-permute-start(bf16[192,256]{1,0:T(8,128)(2,1)} %get-tuple-element.67), channel_id=1, source_target_pairs={{0,24},{4,28},{8,0},{12,4},{16,8},{20,12},{24,16},{28,20},{1,25},{... | collective-permute-start | bytes 294920 | tf_op jit(solution)/shard_map/ppermute | solution.py:609
  211.2 4.8 %bitcast_select_fusion.refs_4_.refs_6_ = bf16[768,3840]{1,0:T(8,128)(2,1)} fusion(pred[768]{0:T(1024)(128)(4,1)S(1)} %iota.144, bf16[2,2,2,2,24,3840]{5,4,3,2,1,0:T(8,128)(2,1)} %collective-permute-done.27, bf16[2,2,2,2,24,3840]{5,4,3,2,1,0:T(8,128)(2,1)S(1)} %broadcast_select_fusion), kind=kLoop, calls=%fused_computation.1 | loop fusion | flops 2949120 | bytes 11797248 | tf_op jit(solution)/shard_map/jit(_where)/select_n | solution.py:100
  218.5 13.6 %middle.1 = (f32[256,768]{1,0:T(8,128)}, bf16[768,256]{1,0:T(8,128)(2,1)}, bf16[256,768]{1,0:T(8,128)(2,1)}, bf16[256,768]{1,0:T(8,128)(2,1)}, f32[256,768]{1,0:...) custom-call(s32[7]{0:T(128)} %pad_add_fusion.where_ref, ...), custom_call_target="tpu_custom_call" | custom-call | flops 5435817984 | bytes 17301504 | tf_op jit(solution)/shard_map/middle/pallas_call | solution.py:486
  255.3 20.7 %attend_back.1 = (bf16[192,256]{1,0:T(8,128)(2,1)}, bf16[192,256]{1,0:T(8,128)(2,1)}, bf16[192,256]{1,0:T(8,128)(2,1)}, bf16[192,256]{1,0:T(8,128)(2,1)}, bf16[3...) custom-call(s32[7]{0:T(128)} %pad_add_fusion.where_ref, ...), custom_call_target="tpu_custom_call" | custom-call | flops 2013265920 | bytes 6291456 | tf_op jit(solution)/shard_map/attend_back/pallas_call | solution.py:340
  277.6 3.5 collective-permute-start.36
  285.1 5.4 %collective-permute-done.37 = bf16[192,256]{1,0:T(8,128)(2,1)S(1)} collective-permute-done((bf16[192,256]{1,0:T(8,128)(2,1)}, bf16[192,256]{1,0:T(8,128)(2,1)S(1)}, u32[]{:S(2)}, u32[]{:S(2)}) %collective-permute-start.37) | collective-permute-done | bytes 98336 | tf_op jit(solution)/shard_map/ppermute | solution.py:609
  294.4 4.1 collective-permute-done.42
  308.2 10.3 %collective-permute-done.43 = bf16[384,256]{1,0:T(8,128)(2,1)S(1)} collective-permute-done((bf16[384,256]{1,0:T(8,128)(2,1)S(1)}, bf16[384,256]{1,0:T(8,128)(2,1)S(1)}, u32[]{:S(2)}, u32[]{:S(2)}) %collective-permute-start.43) | collective-permute-done | bytes 196640 | tf_op jit(solution)/shard_map/ppermute | solution.py:609
  336.4 10.2 %collective-permute-done.52 = bf16[192,1152]{1,0:T(8,128)(2,1)S(1)} collective-permute-done((bf16[192,1152]{1,0:T(8,128)(2,1)S(1)}, bf16[192,1152]{1,0:T(8,128)(2,1)S(1)}, u32[]{:S(2)}, u32[]{:S(2)}) %collective-permute-start.52) | collective-permute-done | bytes 442400 | tf_op jit(solution)/shard_map/ppermute | solution.py:83
  349.9 3.8 collective-permute-done.53
  356.1 3.6 collective-permute-done.54
  380.8 13.8 %collective-permute-done.62 = bf16[2,2,2,96,768]{4,3,0,1,2:T(8,128)(2,1)S(1)} collective-permute-done((bf16[2,2,2,96,768]{4,3,0,1,2:T(8,128)(2,1)}, bf16[2,2,2,96,768]{4,3,0,1,2:T(8,128)(2,1)S(1)}, u32[]{:S(2)}, u32[]{:S(2)}) %collective-permute-start.62) | collective-permute-done | bytes 1179680 | tf_op jit(solution)/shard_map/ppermute | solution.py:83
  396.4 15.0 %collective-permute-done.57 = bf16[192,3840]{1,0:T(8,128)(2,1)} collective-permute-done((bf16[192,3840]{1,0:T(8,128)(2,1)}, bf16[192,3840]{1,0:T(8,128)(2,1)}, u32[]{:S(2)}, u32[]{:S(2)}) %collective-permute-start.57) | collective-permute-done | bytes 1474592 | tf_op jit(solution)/shard_map/ppermute | solution.py:83
  414.9 5.2 %collective-permute-done.63 = bf16[2,2,96,768]{3,2,0,1:T(8,128)(2,1)S(1)} collective-permute-done((bf16[2,2,96,768]{3,2,0,1:T(8,128)(2,1)S(1)}, bf16[2,2,96,768]{3,2,0,1:T(8,128)(2,1)S(1)}, u32[]{:S(2)}, u32[]{:S(2)}) %collective-permute-start.63) | collective-permute-done | bytes 589856 | tf_op jit(solution)/shard_map/ppermute | solution.py:83
  421.0 3.7 collective-permute-done.58
  425.7 5.4 %collective-permute-done.64 = bf16[2,96,768]{2,1,0:T(8,128)(2,1)S(1)} collective-permute-done((bf16[2,96,768]{2,1,0:T(8,128)(2,1)S(1)}, bf16[2,96,768]{2,1,0:T(8,128)(2,1)S(1)}, u32[]{:S(2)}, u32[]{:S(2)}) %collective-permute-start.64) | collective-permute-done | bytes 294944 | tf_op jit(solution)/shard_map/ppermute | solution.py:83
  431.6 4.5 %collective-permute-done.59 = bf16[48,3840]{1,0:T(8,128)(2,1)S(1)} collective-permute-done((bf16[48,3840]{1,0:T(8,128)(2,1)S(1)}, bf16[48,3840]{1,0:T(8,128)(2,1)S(1)}, u32[]{:S(2)}, u32[]{:S(2)}) %collective-permute-start.59) | collective-permute-done | bytes 368672 | tf_op jit(solution)/shard_map/ppermute | solution.py:83
  442.1 3.2 collective-permute-done.60
  (345 shorter events, 163.6 us)
Async XLA Ops:
  2.4 19.2 %collective-permute-start.23 = (bf16[24,3840]{1,0:T(8,128)(2,1)S(1)}, bf16[24,3840]{1,0:T(8,128)(2,1)S(1)}, u32[]{:S(2)}, u32[]{:S(2)}) collective-permute-start(bf16[24,3840]{1,0:T(8,128)(2,1)S(1)} %constant_dynamic-update-slice_fusion), channel_id=1, source_target_pairs={{0,16},{4,20},{8,24},{12,28},{16,0},{20,4},{24,8},{28,12},{1,17},{... | collective-permute-start | bytes 552968 | tf_op jit(solution)/shard_map/ppermute | solution.py:83
  9.1 27.0 %collective-permute-start.5 = (bf16[24,1280]{1,0:T(8,128)(2,1)S(1)}, bf16[24,1280]{1,0:T(8,128)(2,1)S(1)}, u32[]{:S(2)}, u32[]{:S(2)}) collective-permute-start(bf16[24,1280]{1,0:T(8,128)(2,1)S(1)} %fusion.59), channel_id=1, source_target_pairs={{0,16},{4,20},{8,24},{12,28},{16,0},{20,4},{24,8},{28,12},{1,17},{... | collective-permute-start | bytes 184328 | tf_op jit(solution)/shard_map/ppermute | solution.py:83
  9.2 15.0 %collective-permute-start = (bf16[24,1152]{1,0:T(8,128)(2,1)S(1)}, bf16[24,1152]{1,0:T(8,128)(2,1)S(1)}, u32[]{:S(2)}, u32[]{:S(2)}) collective-permute-start(bf16[24,1152]{1,0:T(8,128)(2,1)S(1)} %get-tuple-element.150), channel_id=1, source_target_pairs={{0,16},{4,20},{8,24},{12,28},{16,0},{20,4},{24,8},{28,12},{1,17},{... | collective-permute-start | bytes 165896 | tf_op jit(solution)/shard_map/ppermute | solution.py:83
  12.1 24.2 %collective-permute-start.28 = (bf16[96,768]{1,0:T(8,128)(2,1)}, bf16[96,768]{1,0:T(8,128)(2,1)S(1)}, u32[]{:S(2)}, u32[]{:S(2)}) collective-permute-start(bf16[96,768]{1,0:T(8,128)(2,1)} %param.30), channel_id=1, source_target_pairs={{0,16},{4,20},{8,24},{12,28},{16,0},{20,4},{24,8},{28,12},{1,17},{... | collective-permute-start | bytes 442376 | tf_op jit(solution)/shard_map/ppermute | solution.py:83
  21.7 12.7 %collective-permute-start.24 = (bf16[2,24,3840]{2,1,0:T(8,128)(2,1)S(1)}, bf16[2,24,3840]{2,1,0:T(8,128)(2,1)S(1)}, u32[]{:S(2)}, u32[]{:S(2)}) collective-permute-start(bf16[2,24,3840]{2,1,0:T(8,128)(2,1)S(1)} %broadcast_select_fusion.9), channel_id=1, source_target_pairs={{0,8},{4,12},{8,0},{12,4},{16,24},{20,28},{24,16},{28,20},{1,9},{5... | collective-permute-start | bytes 1105928 | tf_op jit(solution)/shard_map/ppermute | solution.py:83
  24.2 31.1 %collective-permute-start.1 = (bf16[2,24,1152]{2,1,0:T(8,128)(2,1)S(1)}, bf16[2,24,1152]{2,1,0:T(8,128)(2,1)S(1)}, u32[]{:S(2)}, u32[]{:S(2)}) collective-permute-start(bf16[2,24,1152]{2,1,0:T(8,128)(2,1)S(1)} %broadcast_select_fusion.14), channel_id=1, source_target_pairs={{0,8},{4,12},{8,0},{12,4},{16,24},{20,28},{24,16},{28,20},{1,9},{5... | collective-permute-start | bytes 331784 | tf_op jit(solution)/shard_map/ppermute | solution.py:83
  34.5 18.4 %collective-permute-start.25 = (bf16[2,2,24,3840]{3,2,1,0:T(8,128)(2,1)S(1)}, bf16[2,2,24,3840]{3,2,1,0:T(8,128)(2,1)S(1)}, u32[]{:S(2)}, u32[]{:S(2)}) collective-permute-start(bf16[2,2,24,3840]{3,2,1,0:T(8,128)(2,1)S(1)} %broadcast_select_fusion.5), channel_id=1, source_target_pairs={{0,4},{4,0},{8,12},{12,8},{16,20},{20,16},{24,28},{28,24},{1,5},{5... | collective-permute-start | bytes 2211848 | tf_op jit(solution)/shard_map/ppermute | solution.py:83
  36.4 18.3 %collective-permute-start.29 = (bf16[2,96,768]{2,1,0:T(8,128)(2,1)S(1)}, bf16[2,96,768]{2,1,0:T(8,128)(2,1)S(1)}, u32[]{:S(2)}, u32[]{:S(2)}) collective-permute-start(bf16[2,96,768]{2,1,0:T(8,128)(2,1)S(1)} %broadcast_select_fusion.10), channel_id=1, source_target_pairs={{0,8},{4,12},{8,0},{12,4},{16,24},{20,28},{24,16},{28,20},{1,9},{5... | collective-permute-start | bytes 884744 | tf_op jit(solution)/shard_map/ppermute | solution.py:83
  42.6 14.5 %collective-permute-start.7 = (bf16[2,2,24,1280]{3,2,1,0:T(8,128)(2,1)S(1)}, bf16[2,2,24,1280]{3,2,1,0:T(8,128)(2,1)S(1)}, u32[]{:S(2)}, u32[]{:S(2)}) collective-permute-start(bf16[2,2,24,1280]{3,2,1,0:T(8,128)(2,1)S(1)} %broadcast_select_fusion.11), channel_id=1, source_target_pairs={{0,2},{1,3},{2,0},{3,1},{4,6},{5,7},{6,4},{7,5},{8,10},{9,11},{10,... | collective-permute-start | bytes 737288 | tf_op jit(solution)/shard_map/ppermute | solution.py:83
  53.1 47.7 %collective-permute-start.26 = (bf16[2,2,2,24,3840]{4,3,2,1,0:T(8,128)(2,1)S(1)}, bf16[2,2,2,24,3840]{4,3,2,1,0:T(8,128)(2,1)S(1)}, u32[]{:S(2)}, u32[]{:S(2)}) collective-permute-start(bf16[2,2,2,24,3840]{4,3,2,1,0:T(8,128)(2,1)S(1)} %broadcast_select_fusion.1), channel_id=1, source_target_pairs={{0,2},{1,3},{2,0},{3,1},{4,6},{5,7},{6,4},{7,5},{8,10},{9,11},{10,... | collective-permute-start | bytes 4423688 | tf_op jit(solution)/shard_map/ppermute | solution.py:83
  54.8 44.2 %collective-permute-start.30 = (bf16[2,2,96,768]{3,2,1,0:T(8,128)(2,1)S(1)}, bf16[2,2,96,768]{3,2,1,0:T(8,128)(2,1)S(1)}, u32[]{:S(2)}, u32[]{:S(2)}) collective-permute-start(bf16[2,2,96,768]{3,2,1,0:T(8,128)(2,1)S(1)} %broadcast_select_fusion.6), channel_id=1, source_target_pairs={{0,2},{1,3},{2,0},{3,1},{4,6},{5,7},{6,4},{7,5},{8,10},{9,11},{10,... | collective-permute-start | bytes 1769480 | tf_op jit(solution)/shard_map/ppermute | solution.py:83
  55.5 45.7 %collective-permute-start.2 = (bf16[2,2,24,1152]{3,2,1,0:T(8,128)(2,1)S(1)}, bf16[2,2,24,1152]{3,2,1,0:T(8,128)(2,1)S(1)}, u32[]{:S(2)}, u32[]{:S(2)}) collective-permute-start(bf16[2,2,24,1152]{3,2,1,0:T(8,128)(2,1)S(1)} %broadcast_select_fusion.12), channel_id=1, source_target_pairs={{0,4},{4,0},{8,12},{12,8},{16,20},{20,16},{24,28},{28,24},{1,5},{5... | collective-permute-start | bytes 663560 | tf_op jit(solution)/shard_map/ppermute | solution.py:83
  57.2 69.8 %collective-permute-start.8 = (bf16[2,2,2,24,1280]{4,3,2,1,0:T(8,128)(2,1)S(1)}, bf16[2,2,2,24,1280]{4,3,2,1,0:T(8,128)(2,1)S(1)}, u32[]{:S(2)}, u32[]{:S(2)}) collective-permute-start(bf16[2,2,2,24,1280]{4,3,2,1,0:T(8,128)(2,1)S(1)} %broadcast_select_fusion.7), channel_id=1, source_target_pairs={{0,4},{4,0},{8,12},{12,8},{16,20},{20,16},{24,28},{28,24},{1,5},{5... | collective-permute-start | bytes 1474568 | tf_op jit(solution)/shard_map/ppermute | solution.py:83
  99.2 26.1 %collective-permute-start.31 = (bf16[2,2,2,96,768]{4,3,2,1,0:T(8,128)(2,1)S(1)}, bf16[2,2,2,96,768]{4,3,2,1,0:T(8,128)(2,1)S(1)}, u32[]{:S(2)}, u32[]{:S(2)}) collective-permute-start(bf16[2,2,2,96,768]{4,3,2,1,0:T(8,128)(2,1)S(1)} %broadcast_select_fusion.2), channel_id=1, source_target_pairs={{0,4},{4,0},{8,12},{12,8},{16,20},{20,16},{24,28},{28,24},{1,5},{5... | collective-permute-start | bytes 3538952 | tf_op jit(solution)/shard_map/ppermute | solution.py:83
  101.1 110.1 %collective-permute-start.27 = (bf16[2,2,2,2,24,3840]{5,4,3,2,1,0:T(8,128)(2,1)S(1)}, bf16[2,2,2,2,24,3840]{5,4,3,2,1,0:T(8,128)(2,1)}, u32[]{:S(2)}, u32[]{:S(2)}) collective-permute-start(bf16[2,2,2,2,24,3840]{5,4,3,2,1,0:T(8,128)(2,1)S(1)} %broadcast_select_fusion), channel_id=1, source_target_pairs={{0,1},{1,0},{2,3},{3,2},{4,5},{5,4},{6,7},{7,6},{8,9},{9,8},{10,11... | collective-permute-start | bytes 8847368 | tf_op jit(solution)/shard_map/ppermute | solution.py:83
  101.4 27.3 %collective-permute-start.3 = (bf16[2,2,2,24,1152]{4,3,2,1,0:T(8,128)(2,1)S(1)}, bf16[2,2,2,24,1152]{4,3,2,1,0:T(8,128)(2,1)S(1)}, u32[]{:S(2)}, u32[]{:S(2)}) collective-permute-start(bf16[2,2,2,24,1152]{4,3,2,1,0:T(8,128)(2,1)S(1)} %broadcast_select_fusion.8), channel_id=1, source_target_pairs={{0,2},{1,3},{2,0},{3,1},{4,6},{5,7},{6,4},{7,5},{8,10},{9,11},{10,... | collective-permute-start | bytes 1327112 | tf_op jit(solution)/shard_map/ppermute | solution.py:83
  127.0 90.8 %collective-permute-start.32 = (bf16[16,96,768]{2,1,0:T(8,128)(2,1)}, bf16[16,96,768]{2,1,0:T(8,128)(2,1)}, u32[]{:S(2)}, u32[]{:S(2)}) collective-permute-start(bf16[16,96,768]{2,1,0:T(8,128)(2,1)} %bitcast_select_fusion.1.refs_8_), channel_id=1, source_target_pairs={{0,1},{1,0},{2,3},{3,2},{4,5},{5,4},{6,7},{7,6},{8,9},{9,8},{10,11... | collective-permute-start | bytes 7077896 | tf_op jit(solution)/shard_map/ppermute | solution.py:83
  145.6 18.3 %collective-permute-start.13 = (bf16[384,256]{1,0:T(8,128)(2,1)}, bf16[384,256]{1,0:T(8,128)(2,1)S(1)}, u32[]{:S(2)}, u32[]{:S(2)}) collective-permute-start(bf16[384,256]{1,0:T(8,128)(2,1)} %get-tuple-element.63), channel_id=1, source_target_pairs={{0,8},{4,12},{8,16},{12,20},{16,24},{20,28},{24,0},{28,4},{1,9},{5... | collective-permute-start | bytes 589832 | tf_op jit(solution)/shard_map/ppermute | solution.py:609
  147.8 13.2 %collective-permute-start.11 = (bf16[192,256]{1,0:T(8,128)(2,1)}, bf16[192,256]{1,0:T(8,128)(2,1)S(1)}, u32[]{:S(2)}, u32[]{:S(2)}) collective-permute-start(bf16[192,256]{1,0:T(8,128)(2,1)} %get-tuple-element.60), channel_id=1, source_target_pairs={{0,16},{4,20},{8,24},{12,28},{16,0},{20,4},{24,8},{28,12},{1,17},{... | collective-permute-start | bytes 294920 | tf_op jit(solution)/shard_map/ppermute | solution.py:609
  161.0 12.7 %collective-permute-start.15 = (bf16[384,256]{1,0:T(8,128)(2,1)}, bf16[384,256]{1,0:T(8,128)(2,1)}, u32[]{:S(2)}, u32[]{:S(2)}) collective-permute-start(bf16[384,256]{1,0:T(8,128)(2,1)} %get-tuple-element.65), channel_id=1, source_target_pairs={{0,24},{4,28},{8,0},{12,4},{16,8},{20,12},{24,16},{28,20},{1,25},{... | collective-permute-start | bytes 589832 | tf_op jit(solution)/shard_map/ppermute | solution.py:609
  174.7 12.8 %collective-permute-start.19 = (bf16[384,256]{1,0:T(8,128)(2,1)}, bf16[384,256]{1,0:T(8,128)(2,1)}, u32[]{:S(2)}, u32[]{:S(2)}) collective-permute-start(bf16[384,256]{1,0:T(8,128)(2,1)} %collective-permute-done.15.refs_7_), channel_id=1, source_target_pairs={{0,4},{4,0},{8,12},{12,8},{16,20},{20,16},{24,28},{28,24},{1,5},{5... | collective-permute-start | bytes 589832 | tf_op jit(solution)/shard_map/ppermute | solution.py:635
  243.7 119.9 %collective-permute-start.61 = (bf16[2,2,2,2,96,768]{5,4,0,1,3,2:T(8,128)(2,1)}, bf16[2,2,2,2,96,768]{5,4,0,1,3,2:T(8,128)(2,1)}, u32[]{:S(2)}, u32[]{:S(2)}) collective-permute-start(bf16[2,2,2,2,96,768]{5,4,0,1,3,2:T(8,128)(2,1)} %select_bitcast_fusion), channel_id=1, source_target_pairs={{0,1},{1,0},{2,3},{3,2},{4,5},{5,4},{6,7},{7,6},{8,9},{9,8},{10,11... | collective-permute-start | bytes 7077896 | tf_op jit(solution)/shard_map/ppermute | solution.py:83
  276.0 18.3 %collective-permute-start.39 = (bf16[384,256]{1,0:T(8,128)(2,1)}, bf16[384,256]{1,0:T(8,128)(2,1)S(1)}, u32[]{:S(2)}, u32[]{:S(2)}) collective-permute-start(bf16[384,256]{1,0:T(8,128)(2,1)} %get-tuple-element.86), channel_id=1, source_target_pairs={{0,4},{4,0},{8,12},{12,8},{16,20},{20,16},{24,28},{28,24},{1,5},{5... | collective-permute-start | bytes 589832 | tf_op jit(solution)/shard_map/ppermute | solution.py:635
  294.4 76.0 %collective-permute-start.56 = (bf16[384,3840]{1,0:T(8,128)(2,1)}, bf16[384,3840]{1,0:T(8,128)(2,1)}, u32[]{:S(2)}, u32[]{:S(2)}) collective-permute-start(bf16[384,3840]{1,0:T(8,128)(2,1)} %pad_maximum_fusion), channel_id=1, source_target_pairs={{0,1},{1,0},{2,3},{3,2},{4,5},{5,4},{6,7},{7,6},{8,9},{9,8},{10,11... | collective-permute-start | bytes 8847368 | tf_op jit(solution)/shard_map/ppermute | solution.py:83
  301.9 16.7 %collective-permute-start.43 = (bf16[384,256]{1,0:T(8,128)(2,1)S(1)}, bf16[384,256]{1,0:T(8,128)(2,1)S(1)}, u32[]{:S(2)}, u32[]{:S(2)}) collective-permute-start(bf16[384,256]{1,0:T(8,128)(2,1)S(1)} %get-tuple-element.133), channel_id=1, source_target_pairs={{0,16},{4,20},{8,24},{12,28},{16,0},{20,4},{24,8},{28,12},{1,17},{... | collective-permute-start | bytes 589832 | tf_op jit(solution)/shard_map/ppermute | solution.py:609
  303.2 15.4 %collective-permute-start.45 = (bf16[384,256]{1,0:T(8,128)(2,1)S(1)}, bf16[384,256]{1,0:T(8,128)(2,1)S(1)}, u32[]{:S(2)}, u32[]{:S(2)}) collective-permute-start(bf16[384,256]{1,0:T(8,128)(2,1)S(1)} %get-tuple-element.132), channel_id=1, source_target_pairs={{0,8},{4,12},{8,16},{12,20},{16,24},{20,28},{24,0},{28,4},{1,9},{5... | collective-permute-start | bytes 589832 | tf_op jit(solution)/shard_map/ppermute | solution.py:609
  335.1 13.4 %collective-permute-start.47 = (bf16[192,1280]{1,0:T(8,128)(2,1)S(1)}, bf16[192,1280]{1,0:T(8,128)(2,1)S(1)}, u32[]{:S(2)}, u32[]{:S(2)}) collective-permute-start(bf16[192,1280]{1,0:T(8,128)(2,1)S(1)} %slice.383), channel_id=1, source_target_pairs={{0,4},{4,0},{8,12},{12,8},{16,20},{20,16},{24,28},{28,24},{1,5},{5... | collective-permute-start | bytes 1474568 | tf_op jit(solution)/shard_map/ppermute | solution.py:83
  359.7 17.0 %collective-permute-start.55 = (bf16[24,1152]{1,0:T(8,128)(2,1)S(1)}, bf16[24,1152]{1,0:T(8,128)(2,1)S(1)}, u32[]{:S(2)}, u32[]{:S(2)}) collective-permute-start(bf16[24,1152]{1,0:T(8,128)(2,1)S(1)} %slice.401), channel_id=1, source_target_pairs={{0,16},{4,20},{8,24},{12,28},{16,0},{20,4},{24,8},{28,12},{1,17},{... | collective-permute-start | bytes 165896 | tf_op jit(solution)/shard_map/ppermute | solution.py:83
  361.9 15.5 %collective-permute-start.50 = (bf16[24,1280]{1,0:T(8,128)(2,1)S(1)}, bf16[24,1280]{1,0:T(8,128)(2,1)S(1)}, u32[]{:S(2)}, u32[]{:S(2)}) collective-permute-start(bf16[24,1280]{1,0:T(8,128)(2,1)S(1)} %slice.389), channel_id=1, source_target_pairs={{0,16},{4,20},{8,24},{12,28},{16,0},{20,4},{24,8},{28,12},{1,17},{... | collective-permute-start | bytes 184328 | tf_op jit(solution)/shard_map/ppermute | solution.py:83
  368.9 25.8 %collective-permute-start.62 = (bf16[2,2,2,96,768]{4,3,0,1,2:T(8,128)(2,1)}, bf16[2,2,2,96,768]{4,3,0,1,2:T(8,128)(2,1)S(1)}, u32[]{:S(2)}, u32[]{:S(2)}) collective-permute-start(bf16[2,2,2,96,768]{4,3,0,1,2:T(8,128)(2,1)} %select_bitcast_fusion.1), channel_id=1, source_target_pairs={{0,4},{4,0},{8,12},{12,8},{16,20},{20,16},{24,28},{28,24},{1,5},{5... | collective-permute-start | bytes 3538952 | tf_op jit(solution)/shard_map/ppermute | solution.py:83
  375.8 35.5 %collective-permute-start.57 = (bf16[192,3840]{1,0:T(8,128)(2,1)}, bf16[192,3840]{1,0:T(8,128)(2,1)}, u32[]{:S(2)}, u32[]{:S(2)}) collective-permute-start(bf16[192,3840]{1,0:T(8,128)(2,1)} %slice.410), channel_id=1, source_target_pairs={{0,2},{1,3},{2,0},{3,1},{4,6},{5,7},{6,4},{7,5},{8,10},{9,11},{10,... | collective-permute-start | bytes 4423688 | tf_op jit(solution)/shard_map/ppermute | solution.py:83
  395.2 24.8 %collective-permute-start.63 = (bf16[2,2,96,768]{3,2,0,1:T(8,128)(2,1)S(1)}, bf16[2,2,96,768]{3,2,0,1:T(8,128)(2,1)S(1)}, u32[]{:S(2)}, u32[]{:S(2)}) collective-permute-start(bf16[2,2,96,768]{3,2,0,1:T(8,128)(2,1)S(1)} %select_bitcast_fusion.2), channel_id=1, source_target_pairs={{0,2},{1,3},{2,0},{3,1},{4,6},{5,7},{6,4},{7,5},{8,10},{9,11},{10,... | collective-permute-start | bytes 1769480 | tf_op jit(solution)/shard_map/ppermute | solution.py:83
  (82 other events, 783.2 us)
